TPU v7x, 32 devices: a whole 2x2x4 slice. The times are simulated.
32 devices in a mesh: dp: 8 (over z, y), tensor: 4 (over x, core).
Axes of the slice: x: 2, y: 2, z: 4, core: 2. Of those that a mesh axis runs over, the one named last changes fastest.
Arguments:
- tokens: bfloat16 [8192, 768], P('dp'), may hold values from -6 to 6
- segment_ids: int32 [16, 512], P('dp'), may hold values from 0 to 3, never falling along the last dimension, each value on 1 to 256 neighbouring positions
- qkv_weight: bfloat16 [768, 3, 12, 64], P(None, None, 'tensor'), may hold values from -0.21875 to 0.21875
- qkv_bias: bfloat16 [2, 12, 64], P(None, 'tensor'), may hold values from -3 to 3
- output_weight: bfloat16 [12, 64, 768], P('tensor'), may hold values from -1.25 to 1.25
- output_bias: bfloat16 [768], replicated, may hold values from -2 to 2
- first_gain: bfloat16 [768], replicated, may hold values from 0.5 to 1.5
- first_shift: bfloat16 [768], replicated, may hold values from -2 to 2
- up_weight: bfloat16 [768, 3072], P(None, 'tensor'), may hold values from -0.21875 to 0.21875
- up_bias: bfloat16 [48, 64], P('tensor'), may hold values from -3 to 3
- down_weight: bfloat16 [3072, 768], P('tensor'), may hold values from -0.109375 to 0.109375
- down_bias: bfloat16 [768], replicated, may hold values from -2 to 2
- second_gain: bfloat16 [768], replicated, may hold values from 0.5 to 1.5
- second_shift: bfloat16 [768], replicated, may hold values from -2 to 2
- cotangent: bfloat16 [8192, 768], P('dp'), may hold values from -6 to 6
Outputs:
- layer_out: bfloat16 [8192, 768], P(('dp', 'tensor'))
- tokens_grad: bfloat16 [8192, 768], P(('dp', 'tensor'))
- qkv_weight_grad: float32 [768, 3, 12, 64], P('dp', None, 'tensor')
- qkv_bias_grad: float32 [2, 12, 64], P(None, 'tensor', 'dp')
- output_weight_grad: float32 [12, 64, 768], P('tensor', None, 'dp')
- output_bias_grad: float32 [768], P('dp')
- first_gain_grad: float32 [768], P('dp')
- first_shift_grad: float32 [768], P('dp')
- up_weight_grad: float32 [768, 3072], P('dp', 'tensor')
- up_bias_grad: float32 [48, 64], P('tensor', 'dp')
- down_weight_grad: float32 [3072, 768], P('tensor', 'dp')
- down_bias_grad: float32 [768], P('dp')
- second_gain_grad: float32 [768], P('dp')
- second_shift_grad: float32 [768], P('dp')
Inputs may be any that keep to these rules, and one draw needn't show every extreme that they name: `segment_ids`: along each row of 512 tokens the ids never fall; each id covers 1 to 256 tokens of its row.
All inputs are finite; a program needn't handle non-finite values.
Results may differ from a plain program's by a relative error of at most 0.02.
The roundings to bfloat16 on the way count: a program that leaves them out, or rounds other values in their place, can miss the bound.
Values may be sent and summed in bfloat16 or wider, within the bound.
A program may use at most 128 MiB of HBM per device.

v0:
```python
import jax
import jax.numpy as jnp
from jax import lax
from jax.sharding import PartitionSpec as P

HEAD = 64
SEQ = 512


EPS = 1e-12


def normalize(rows_in, gain_vec, shift_vec):
    center = rows_in - jnp.mean(rows_in, axis=-1, keepdims=True)
    spread = jnp.mean(center * center, axis=-1, keepdims=True)
    return center * lax.rsqrt(spread + EPS) * gain_vec + shift_vec


def norm_back(rows_in, gain_vec, shift_vec, grad_out):
    unused, pull_back = jax.vjp(normalize, rows_in, gain_vec, shift_vec)
    return pull_back(grad_out)


def gelu_exact(values_in):
    return jax.nn.gelu(values_in, approximate=False)


def head_scores(queries, keys_low, same_doc):
    scores = jnp.einsum(
        "rqhd,rkhd->rhqk", queries, keys_low, preferred_element_type=jnp.float32
    ) * HEAD ** (-0.5)
    return jnp.where(same_doc[:, None], scores, -1e30)


def attend(queries, keys_low, values_low, same_doc):
    scores = head_scores(queries, keys_low, same_doc)
    row_top = jnp.max(scores, axis=-1, keepdims=True)
    expo_vals = jnp.exp(scores - row_top)
    row_total = jnp.sum(expo_vals, axis=-1, keepdims=True)
    attn_probs = (expo_vals / row_total).astype(jnp.bfloat16)
    context = jnp.einsum(
        "rhqk,rkhd->rqhd", attn_probs, values_low, preferred_element_type=jnp.float32
    )
    return (context.astype(jnp.bfloat16), row_top + jnp.log(row_total))


def attend_back(queries, keys_low, values_low, same_doc, log_total, d_context):
    probs_full = jnp.exp(head_scores(queries, keys_low, same_doc) - log_total)
    d_probs = jnp.einsum(
        "rqhd,rkhd->rhqk", d_context, values_low, preferred_element_type=jnp.float32
    )
    inner_sum = jnp.sum(probs_full * d_probs, axis=-1, keepdims=True)
    d_scores = (probs_full * (d_probs - inner_sum)).astype(jnp.bfloat16)
    factor = HEAD ** (-0.5)
    d_query = (
        jnp.einsum("rhqk,rkhd->rqhd", d_scores, keys_low, preferred_element_type=jnp.float32)
        * factor
    )
    d_keys = (
        jnp.einsum("rhqk,rqhd->rkhd", d_scores, queries, preferred_element_type=jnp.float32)
        * factor
    )
    d_values = jnp.einsum(
        "rhqk,rqhd->rkhd",
        probs_full.astype(jnp.bfloat16),
        d_context,
        preferred_element_type=jnp.float32,
    )
    return (d_query, d_keys, d_values)


def body(
    tokens,
    segment_ids,
    qkv_weight,
    qkv_bias,
    output_weight,
    output_bias,
    first_gain,
    first_shift,
    up_weight,
    up_bias,
    down_weight,
    down_bias,
    second_gain,
    second_shift,
    cotangent,
):
    token_count = tokens.shape[0]
    row_count = token_count // SEQ
    head_count = qkv_weight.shape[2]
    head_width = head_count * HEAD
    share_rows = token_count // lax.axis_size("tensor")
    offset = lax.axis_index("tensor") * share_rows
    same_doc = segment_ids[:, :, None] == segment_ids[:, None, :]
    qkv_matrix = qkv_weight.reshape(qkv_weight.shape[0], 3 * head_width)
    out_matrix = output_weight.reshape(head_width, output_weight.shape[2])
    bias_rows = qkv_bias.astype(jnp.float32).reshape(2, head_width)
    gain_first = first_gain.astype(jnp.float32)
    shift_first = first_shift.astype(jnp.float32)
    gain_second = second_gain.astype(jnp.float32)
    shift_second = second_shift.astype(jnp.float32)

    def split_heads(matrix):
        return matrix.reshape(row_count, SEQ, head_count, HEAD)

    mixed_proj = jnp.dot(tokens, qkv_matrix, preferred_element_type=jnp.float32).reshape(
        token_count, 3, head_width
    )
    queries = (mixed_proj[:, 0] + bias_rows[0]).astype(jnp.bfloat16)
    keys_low = mixed_proj[:, 1].astype(jnp.bfloat16)
    values_low = (mixed_proj[:, 2] + bias_rows[1]).astype(jnp.bfloat16)
    context, log_total = attend(
        split_heads(queries), split_heads(keys_low), split_heads(values_low), same_doc
    )
    context = context.reshape(token_count, head_width)
    attn_terms = jnp.dot(context, out_matrix, preferred_element_type=jnp.float32)
    attn_total = lax.psum(attn_terms.astype(jnp.bfloat16), "tensor").astype(jnp.float32)
    residual = tokens.astype(jnp.float32)
    grad_rows = cotangent.astype(jnp.float32)
    first_in = residual + attn_total + output_bias.astype(jnp.float32)
    first_out = normalize(first_in, gain_first, shift_first)
    first_low = first_out.astype(jnp.bfloat16)
    hidden = jnp.dot(first_low, up_weight, preferred_element_type=jnp.float32) + up_bias.astype(
        jnp.float32
    ).reshape(-1)
    active, gelu_pull = jax.vjp(gelu_exact, hidden)
    active_low = active.astype(jnp.bfloat16)
    down_terms = jnp.dot(active_low, down_weight, preferred_element_type=jnp.float32)
    down_total = lax.psum(down_terms.astype(jnp.bfloat16), "tensor").astype(jnp.float32)
    second_in = first_out + down_total + down_bias.astype(jnp.float32)
    layer_full = normalize(second_in, gain_second, shift_second).astype(jnp.bfloat16)
    d_second, gain_second_grad, shift_second_grad = norm_back(
        second_in, gain_second, shift_second, grad_rows
    )
    down_bias_grad = jnp.sum(d_second, axis=0)
    d_second_low = d_second.astype(jnp.bfloat16)
    down_grad = jnp.einsum(
        "tf,td->fd", active_low, d_second_low, preferred_element_type=jnp.float32
    )
    d_active = jnp.einsum(
        "td,fd->tf", d_second_low, down_weight, preferred_element_type=jnp.float32
    )
    (d_hidden,) = gelu_pull(d_active)
    up_bias_grad = jnp.sum(d_hidden, axis=0).reshape(up_bias.shape)
    d_hidden_low = d_hidden.astype(jnp.bfloat16)
    up_grad = jnp.einsum("td,tf->df", first_low, d_hidden_low, preferred_element_type=jnp.float32)
    up_terms = jnp.einsum("tf,df->td", d_hidden_low, up_weight, preferred_element_type=jnp.float32)
    up_total = lax.psum(up_terms.astype(jnp.bfloat16), "tensor").astype(jnp.float32)
    d_first = d_second + up_total
    d_first_in, gain_first_grad, shift_first_grad = norm_back(
        first_in, gain_first, shift_first, d_first
    )
    out_bias_grad = jnp.sum(d_first_in, axis=0)
    d_attn_low = d_first_in.astype(jnp.bfloat16)
    out_grad = jnp.einsum("tc,td->cd", context, d_attn_low, preferred_element_type=jnp.float32)
    d_context = jnp.einsum(
        "td,cd->tc", d_attn_low, out_matrix, preferred_element_type=jnp.float32
    ).astype(jnp.bfloat16)
    d_query, d_keys, d_values = attend_back(
        split_heads(queries),
        split_heads(keys_low),
        split_heads(values_low),
        same_doc,
        log_total,
        split_heads(d_context),
    )
    d_query = d_query.reshape(token_count, head_width)
    d_keys = d_keys.reshape(token_count, head_width)
    d_values = d_values.reshape(token_count, head_width)
    qkv_bias_grad = jnp.stack([jnp.sum(d_query, axis=0), jnp.sum(d_values, axis=0)]).reshape(
        qkv_bias.shape
    )
    d_mixed = (
        jnp.stack([d_query, d_keys, d_values], axis=1)
        .astype(jnp.bfloat16)
        .reshape(token_count, 3 * head_width)
    )
    qkv_grad = jnp.einsum("td,tc->dc", tokens, d_mixed, preferred_element_type=jnp.float32).reshape(
        qkv_weight.shape
    )
    token_terms = jnp.einsum("tc,dc->td", d_mixed, qkv_matrix, preferred_element_type=jnp.float32)
    token_total = lax.psum(token_terms.astype(jnp.bfloat16), "tensor").astype(jnp.float32)
    tokens_grad = lax.dynamic_slice_in_dim(d_first_in + token_total, offset, share_rows, 0).astype(
        jnp.bfloat16
    )
    layer_out = lax.dynamic_slice_in_dim(layer_full, offset, share_rows, 0)
    small_grads = (
        out_bias_grad,
        gain_first_grad,
        shift_first_grad,
        down_bias_grad,
        gain_second_grad,
        shift_second_grad,
    )
    attn_parts = (
        lax.psum_scatter(qkv_grad, "dp", scatter_dimension=0, tiled=True),
        lax.psum_scatter(qkv_bias_grad, "dp", scatter_dimension=2, tiled=True),
        lax.psum_scatter(
            out_grad.reshape(output_weight.shape), "dp", scatter_dimension=2, tiled=True
        ),
        lax.psum_scatter(small_grads[0], "dp", scatter_dimension=0, tiled=True),
        lax.psum_scatter(small_grads[1], "dp", scatter_dimension=0, tiled=True),
        lax.psum_scatter(small_grads[2], "dp", scatter_dimension=0, tiled=True),
    )
    ffn_parts = (
        lax.psum_scatter(up_grad, "dp", scatter_dimension=0, tiled=True),
        lax.psum_scatter(up_bias_grad, "dp", scatter_dimension=1, tiled=True),
        lax.psum_scatter(down_grad, "dp", scatter_dimension=1, tiled=True),
        lax.psum_scatter(small_grads[3], "dp", scatter_dimension=0, tiled=True),
        lax.psum_scatter(small_grads[4], "dp", scatter_dimension=0, tiled=True),
        lax.psum_scatter(small_grads[5], "dp", scatter_dimension=0, tiled=True),
    )
    return (
        layer_out,
        tokens_grad,
        attn_parts[0],
        attn_parts[1],
        attn_parts[2],
        attn_parts[3],
        attn_parts[4],
        attn_parts[5],
        ffn_parts[0],
        ffn_parts[1],
        ffn_parts[2],
        ffn_parts[3],
        ffn_parts[4],
        ffn_parts[5],
    )


def solution(mesh):
    placed = (
        P("dp", None),
        P("dp", None),
        P(None, None, "tensor", None),
        P(None, "tensor", None),
        P("tensor", None, None),
        P(),
        P(),
        P(),
        P(None, "tensor"),
        P("tensor", None),
        P("tensor", None),
        P(),
        P(),
        P(),
        P("dp", None),
    )
    return jax.shard_map(
        body,
        mesh=mesh,
        in_specs=placed,
        out_specs=(
            P(("dp", "tensor"), None),
            P(("dp", "tensor"), None),
            P("dp", None, "tensor", None),
            P(None, "tensor", "dp"),
            P("tensor", None, "dp"),
            P("dp"),
            P("dp"),
            P("dp"),
            P("dp", "tensor"),
            P("tensor", "dp"),
            P("tensor", "dp"),
            P("dp"),
            P("dp"),
            P("dp"),
        ),
        check_vma=False,
    )
```

profile of v0, /device:TPU:0, one launch (start us, length us, event | category | flops | bytes accessed | tf_op | source)
XLA Modules:
  0.0 553.8 jit_solution(17935516750213851059)
XLA Ops:
  7.2 2.8 fusion.21
  10.2 1.0 fusion.64
  11.2 1.2 broadcast_compare_fusion
  13.4 2.1 squeeze.8
  15.5 2.5 fusion.66
  19.0 1.6 copy-done.2
  20.7 1.3 fusion.29
  23.3 1.9 convolution_convert_fusion.3
  25.5 1.3 convert_element_type.130
  27.4 43.5 %all-reduce.14.cloned.1.call-done = bf16[1024,768]{1,0:T(8,128)(2,1)} async-done(((bf16[1024,768]{1,0:T(8,128)(2,1)}), bf16[1024,768]{1,0:T(8,128)(2,1)}) %all-reduce.14.cloned.1.call-update) | async-done | bytes 1572880 | tf_op jit(solution)/shard_map/psum | solution.py:118
  70.9 2.1 fusion.17
  74.6 9.9 %multiply_convert_fusion.1 = (bf16[1024,768]{1,0:T(8,128)(2,1)S(1)}, f32[1024,768]{1,0:T(8,128)}, f32[1024,768]{1,0:T(8,128)}) fusion(f32[768]{0:T(1024)S(1)} %copy-done.57, bf16[768,768]{1,0:T(8,128)(2,1)S(1)} %copy-done, f32[768]{0:T(1024)S(1)} %copy-done.47, f32[768]{0:T(1024)S(1)} %convert_element_type.129, f32[1024]{0:T(1024)S(1)} %fusion.49, ...), kind=kOutput, calls=%fused_computation.27 | convolution fusion | flops 1266941952 | bytes 12210176 | tf_op jit(solution)/shard_map/dot_general | solution.py:124
  84.5 1.2 copy-done.65
  85.7 2.5 convolution_convert_fusion.2
  88.3 1.3 convert_element_type.136
  89.6 1.3 convert_element_type.135
  90.9 40.5 %all-reduce.16.cloned.1.call-done = bf16[1024,768]{1,0:T(8,128)(2,1)} async-done(((bf16[1024,768]{1,0:T(8,128)(2,1)}), bf16[1024,768]{1,0:T(8,128)(2,1)}) %all-reduce.16.cloned.1.call-update) | async-done | bytes 1572880 | tf_op jit(solution)/shard_map/psum | solution.py:130
  131.4 3.3 fusion.62
  134.7 1.8 fusion.4
  136.5 3.6 fusion.61
  140.8 3.2 fusion.69
  144.0 1.2 copy-done.68
  145.2 2.6 convolution_convert_fusion.1
  148.7 42.2 %all-reduce.18.cloned.1.call-done = bf16[1024,768]{1,0:T(8,128)(2,1)} async-done(((bf16[1024,768]{1,0:T(8,128)(2,1)}), bf16[1024,768]{1,0:T(8,128)(2,1)}) %all-reduce.18.cloned.1.call-update) | async-done | bytes 1572880 | tf_op jit(solution)/shard_map/psum | solution.py:149
  190.9 4.5 fusion.59
  195.4 2.6 multiply_reduce_fusion.1
  198.1 2.1 fusion.60
  200.2 1.8 copy-done.6
  202.9 5.4 fusion.67
  208.3 4.5 multiply_reduce_fusion
  212.9 1.8 multiply_convert_fusion
  214.7 1.1 fusion.26
  219.8 3.8 convolution_convert_fusion
  223.7 2.4 fusion.19
  226.0 1.5 copy.79
  227.6 2.8 reshape.190
  230.4 2.3 convolution_bitcast_fusion
  232.8 3.0 copy.83
  236.0 5.4 fusion.51
  241.5 5.2 fusion.37
  248.8 2.0 fusion.32
  250.8 37.5 %all-reduce.8 = (f32[2,3,64]{2,1,0:T(4,128)S(1)}, f32[768]{0:T(1024)S(1)}, f32[768]{0:T(1024)S(1)}, f32[768]{0:T(1024)S(1)}, f32[12,64]{1,0:T(8,128)S(1)}, /*ind...) all-reduce(f32[2,3,64]{2,1,0:T(4,128)S(1)} %pad_maximum_fusion, ...), channel_id=3, replica_groups=mesh['dp'=8,'tensor'=4] {'dp'}, use_global_device_ids=true, to_apply=%region_18.19.clone | all-reduce | flops 5760 | bytes 46080
  293.2 2.1 fusion.30
  295.3 37.2 %reduce-scatter.17.cloned.1.call-done = f32[96,192]{1,0:T(8,128)} async-done(((f32[768,192]{1,0:T(8,128)}), f32[96,192]{1,0:T(8,128)}) %reduce-scatter.17.cloned.1.call-update) | async-done | bytes 73744
  334.2 67.8 %reduce-scatter.15.cloned.1.call-done = f32[96,576]{1,0:T(8,128)} async-done(((f32[768,576]{1,0:T(8,128)}), f32[96,576]{1,0:T(8,128)}) %reduce-scatter.15.cloned.1.call-update) | async-done | bytes 221200
  402.0 1.8 copy.84
  403.8 70.4 %reduce-scatter.13.cloned.1.call-done = f32[768,96]{0,1:T(8,128)} async-done(((f32[768,768]{0,1:T(8,128)}), f32[768,96]{0,1:T(8,128)}) %reduce-scatter.13.cloned.1.call-update) | async-done | bytes 294928 | tf_op jit(solution)/shard_map/reduce_scatter | solution.py:209
  474.2 72.3 %reduce-scatter.11.cloned.1.call-done = f32[96,768]{1,0:T(8,128)} async-done(((f32[768,768]{1,0:T(8,128)}), f32[96,768]{1,0:T(8,128)}) %reduce-scatter.11.cloned.1.call-update) | async-done | bytes 294928 | tf_op jit(solution)/shard_map/reduce_scatter | solution.py:207
  (202 shorter events, 19.9 us)
Async XLA Ops:
  7.2 67.4 %copy-start = (bf16[768,768]{1,0:T(8,128)(2,1)S(1)}, bf16[768,768]{1,0:T(8,128)(2,1)}, u32[]{:S(2)}) copy-start(bf16[768,768]{1,0:T(8,128)(2,1)} %param.23) | copy-start | bytes 3538948
  7.2 63.7 %all-reduce.14.cloned.1.call-start = ((), (), s32[]{:S(2)}) async-start(), calls=%async_computation.4 | async-start | bytes 3145728 | tf_op jit(solution)/shard_map/psum | solution.py:118
  12.7 5.3 copy-start.9
  13.4 5.6 %copy-start.13 = (f32[2,512,3,64]{1,0,3,2:T(2,128)}, f32[2,512,3,64]{1,0,3,2:T(2,128)S(1)}, u32[]{:S(2)}) copy-start(f32[2,512,3,64]{1,0,3,2:T(2,128)S(1)} %squeeze.7) | copy-start | bytes 2359300
  22.1 4.7 copy-start.56
  22.1 48.8 %copy-start.3 = (bf16[1024,768]{1,0:T(8,128)(2,1)S(1)}, bf16[1024,768]{1,0:T(8,128)(2,1)}, u32[]{:S(2)}) copy-start(bf16[1024,768]{1,0:T(8,128)(2,1)} %param.15) | copy-start | bytes 4718596
  25.2 106.1 %all-reduce.16.cloned.1.call-start = ((), (), s32[]{:S(2)}) async-start(), calls=%async_computation.5 | async-start | bytes 3145728 | tf_op jit(solution)/shard_map/psum | solution.py:130
  25.5 105.9 %copy-start.20 = (f32[768]{0:T(1024)}, f32[768]{0:T(1024)S(1)}, u32[]{:S(2)}) copy-start(f32[768]{0:T(1024)S(1)} %convert_element_type.128) | copy-start | bytes 9220
  25.5 105.8 %copy-start.27 = (f32[768]{0:T(1024)}, f32[768]{0:T(1024)S(1)}, u32[]{:S(2)}) copy-start(f32[768]{0:T(1024)S(1)} %convert_element_type.129) | copy-start | bytes 9220
  73.0 58.3 %copy-start.23 = (f32[1024]{0:T(1024)}, f32[1024]{0:T(1024)S(1)}, u32[]{:S(2)}) copy-start(f32[1024]{0:T(1024)S(1)} %broadcast_multiply_fusion.1) | copy-start | bytes 12292
  74.6 56.8 %copy-start.30 = (f32[1024]{0:T(1024)}, f32[1024]{0:T(1024)S(1)}, u32[]{:S(2)}) copy-start(f32[1024]{0:T(1024)S(1)} %fusion.49) | copy-start | bytes 12292
  74.6 11.1 %copy-start.62 = (bf16[768,768]{1,0:T(8,128)(2,1)S(1)}, bf16[768,768]{1,0:T(8,128)(2,1)}, u32[]{:S(2)}) copy-start(bf16[768,768]{1,0:T(8,128)(2,1)} %param.25) | copy-start | bytes 3538948
  88.3 102.6 %all-reduce.18.cloned.1.call-start = ((), (), s32[]{:S(2)}) async-start(), calls=%async_computation.6 | async-start | bytes 3145728 | tf_op jit(solution)/shard_map/psum | solution.py:149
  136.5 4.3 copy-start.67
  140.1 4.0 copy-start.7
  140.1 4.0 copy-start.49
  147.8 145.4 %all-reduce.20.cloned.1.call-start = ((), (), s32[]{:S(2)}) async-start(), calls=%async_computation.7 | async-start | bytes 3145728 | tf_op jit(solution)/shard_map/psum | solution.py:183
  148.6 46.8 %copy-start.39 = (f32[1024]{0:T(1024)S(1)}, f32[1024]{0:T(1024)}, u32[]{:S(2)}) copy-start(f32[1024]{0:T(1024)} %copy-done.38) | copy-start | bytes 12292
  148.6 46.8 %copy-start.21 = (f32[768]{0:T(1024)S(1)}, f32[768]{0:T(1024)}, u32[]{:S(2)}) copy-start(f32[768]{0:T(1024)} %copy-done.20) | copy-start | bytes 9220
  148.6 46.8 %copy-start.24 = (f32[1024]{0:T(1024)S(1)}, f32[1024]{0:T(1024)}, u32[]{:S(2)}) copy-start(f32[1024]{0:T(1024)} %copy-done.23) | copy-start | bytes 12292
  148.6 46.8 %copy-start.28 = (f32[768]{0:T(1024)S(1)}, f32[768]{0:T(1024)}, u32[]{:S(2)}) copy-start(f32[768]{0:T(1024)} %copy-done.27) | copy-start | bytes 9220
  148.7 46.8 %copy-start.31 = (f32[1024]{0:T(1024)S(1)}, f32[1024]{0:T(1024)}, u32[]{:S(2)}) copy-start(f32[1024]{0:T(1024)} %copy-done.30) | copy-start | bytes 12292
  190.9 4.5 copy-start.5
  202.9 5.4 copy-start.14
  202.9 5.4 copy-start.41
  202.9 9.9 %slice-start = ((s8[6291456]{0:T(1024)(128)(4,1)}), s8[4194304]{0:T(1024)(128)(4,1)S(1)}, s32[]{:S(2)}) async-start(s8[6291456]{0:T(1024)(128)(4,1)} %bitcast.84), calls=%async_computation.12 | async-start | bytes 8388608
  208.3 4.6 slice-start.1
  223.6 108.8 %reduce-scatter.17.cloned.1.call-start = ((), (), s32[]{:S(2)}) async-start(), calls=%async_computation.11 | async-start | bytes 884736
  230.4 171.6 %reduce-scatter.15.cloned.1.call-start = ((), (), s32[]{:S(2)}) async-start(), calls=%async_computation.10 | async-start | bytes 2211840
  235.8 5.6 %copy-start.22 = (f32[768]{0:T(1024)S(1)}, f32[768]{0:T(1024)}, u32[]{:S(2)}) copy-start(f32[768]{0:T(1024)} %copy-done.20) | copy-start | bytes 9220
  235.9 5.6 %copy-start.25 = (f32[1024]{0:T(1024)S(1)}, f32[1024]{0:T(1024)}, u32[]{:S(2)}) copy-start(f32[1024]{0:T(1024)} %copy-done.23) | copy-start | bytes 12292
  235.9 5.6 %copy-start.29 = (f32[768]{0:T(1024)S(1)}, f32[768]{0:T(1024)}, u32[]{:S(2)}) copy-start(f32[768]{0:T(1024)} %copy-done.27) | copy-start | bytes 9220
  235.9 5.6 %copy-start.32 = (f32[1024]{0:T(1024)S(1)}, f32[1024]{0:T(1024)}, u32[]{:S(2)}) copy-start(f32[1024]{0:T(1024)} %copy-done.30) | copy-start | bytes 12292
  235.9 5.6 %copy-start.48 = (f32[768]{0:T(1024)S(1)}, f32[768]{0:T(1024)}, u32[]{:S(2)}) copy-start(f32[768]{0:T(1024)} %convert_element_type.130) | copy-start | bytes 9220
  235.9 238.3 %reduce-scatter.13.cloned.1.call-start = ((), (), s32[]{:S(2)}) async-start(), calls=%async_computation.9 | async-start | bytes 2654208 | tf_op jit(solution)/shard_map/reduce_scatter | solution.py:209
  241.4 5.5 copy-start.64
  241.4 7.3 %copy-start.61 = (bf16[768]{0:T(1024)(128)(2,1)S(1)}, bf16[768]{0:T(1024)(128)(2,1)}, u32[]{:S(2)}) copy-start(bf16[768]{0:T(1024)(128)(2,1)} %param.28) | copy-start | bytes 4612
  241.4 7.3 %copy-start.55 = (f32[768]{0:T(1024)S(1)}, f32[768]{0:T(1024)}, u32[]{:S(2)}) copy-start(f32[768]{0:T(1024)} %get-tuple-element.86) | copy-start | bytes 9220
  241.4 7.4 %copy-start.35 = (f32[768]{0:T(1024)S(1)}, f32[768]{0:T(1024)}, u32[]{:S(2)}) copy-start(f32[768]{0:T(1024)} %convert_element_type.136) | copy-start | bytes 9220
  241.4 305.1 %reduce-scatter.11.cloned.1.call-start = ((), (), s32[]{:S(2)}) async-start(), calls=%async_computation.8 | async-start | bytes 2654208 | tf_op jit(solution)/shard_map/reduce_scatter | solution.py:207
  246.7 4.0 copy-start.53
  246.7 4.0 copy-start.42
  246.7 4.1 copy-start.44
  246.7 4.1 copy-start.45
  246.7 4.1 copy-start.46
  246.8 4.1 copy-start.51
  246.8 4.1 copy-start.52
  246.8 299.8 %copy-start.1 = (bf16[768,768]{1,0:T(8,128)(2,1)S(1)}, bf16[768,768]{1,0:T(8,128)(2,1)}, u32[]{:S(2)}) copy-start(bf16[768,768]{1,0:T(8,128)(2,1)} %param.23) | copy-start | bytes 3538948
  (31 other events, 76.6 us)
Sparse Core Ops, SparseCore 0:
  25.3 45.5 all-reduce.13
  88.4 42.9 all-reduce.15
  147.9 42.9 all-reduce.17
  223.7 42.8 all-reduce.19
  269.8 62.5 reduce-scatter.16
  336.1 65.7 reduce-scatter.14
  406.1 68.1 reduce-scatter.12
  478.3 68.2 reduce-scatter.10
where the time goes:
time: 560 us; the launch traced here: 554 us
  waiting for transfers between devices  374 us (67%)
  matrix products  58.2 us (10%)
  blocking collectives  37.5 us (7%)
  other arithmetic  33.5 us (6%)
  local copies, waits for them, and re-layouts  33.3 us (6%)
  between operations  16.9 us (3%)
    unnamed x10, waiting for transfers between devices  105 us
    reduce_scatter x1, waiting for transfers between devices, body(): lax.psum_scatter(up_grad, 'dp', scatter_dimension=0, tiled=True)  72.3 us
    reduce_scatter x1, waiting for transfers between devices, body(): lax.psum_scatter(down_grad, 'dp', scatter_dimension=1, tiled=True)  70.4 us
    psum x1, waiting for transfers between devices, body(): lax.psum(attn_terms.astype(jnp.bfloat16), 'tensor').astype(jnp.float32)  43.5 us
    psum x1, waiting for transfers between devices, body(): lax.psum(up_terms.astype(jnp.bfloat16), 'tensor').astype(jnp.float32)  42.2 us
    psum x1, waiting for transfers between devices, body(): lax.psum(down_terms.astype(jnp.bfloat16), 'tensor').astype(jnp.float32)  40.5 us
    unnamed x1, blocking collectives  37.5 us
    unnamed x161, local copies, waits for them, and re-layouts  25.7 us
  transfers between devices with their start and end apart: 8, of which 7 were waited for; matrix products, arithmetic and copies ran while one was open for 7% of the time, Pallas kernels for 0%

commit v1 on v0

v1 whole, which is shorter than its diff:
```python
import jax
import jax.numpy as jnp
from jax import lax
from jax.experimental import pallas as pl
from jax.experimental.pallas import tpu as pltpu
from jax.sharding import PartitionSpec as P

HEAD = 64
SEQ = 512
EPS = 1e-12
SCALE = HEAD ** (-0.5)
BF = jnp.bfloat16
F32 = jnp.float32
MESH_ID = pl.DeviceIdType.MESH
NAMES = ("dp", "tensor")
PIECES = (
    ("d0", 256),
    ("d1", 256),
    ("d2", 256),
    ("u0", 256),
    ("u1", 256),
    ("u2", 256),
    ("o", 128),
    ("q", 384),
    ("r", 256),
)


def dot(left, right, left_dim, right_dim):
    return lax.dot_general(
        left, right, (((left_dim,), (right_dim,)), ((), ())), preferred_element_type=F32
    )


def mean_of(values):
    return jnp.mean(values, axis=-1, keepdims=True)


def row_sum(values):
    return jnp.sum(values, axis=0, keepdims=True)


def scratch_plan(rows, half, fused):
    plan = {
        "tok": ((rows, 2, 2, 128, 768), BF),
        "cot": ((rows, 2, 128, 768), BF),
        "wq": ((5, 128, 768), BF),
        "wo": ((4, 256, 768), BF),
        "wu": ((768, 768), BF),
        "wd": ((768, 768), BF),
        "mix": ((rows, 512, 640), BF),
        "bias": ((512, 512), F32),
        "prob": ((rows, 3, 512, 512), F32),
        "ctx": ((rows, 512, 256), BF),
        "cs": ((rows, 2, 384, 128), BF),
        "cr": ((rows, 4, 384, 128), BF),
        "n1": ((rows, 256, 768), F32),
        "r1": ((rows, 256, 1), F32),
        "fo": ((rows, 256, 768), F32),
        "flow": ((rows, 2, 2, 128, 768), BF),
        "act": ((rows, 2, 256, 768), BF),
        "gp": ((rows, 2, 256, 768), F32),
        "p2": ((rows, 2, 2, 128, 768), BF),
        "p2r": ((rows, 2, 128, 768), BF),
        "x2": ((rows, 2, 128, 768), BF),
        "x2r": ((rows, 2, 128, 768), BF),
        "ds": ((rows, 256, 768), F32),
        "dsl": ((rows, 2, 2, 128, 768), BF),
        "dhl": ((rows, 2, 256, 768), BF),
        "p3": ((rows, 2, 2, 128, 768), BF),
        "p3r": ((rows, 2, 128, 768), BF),
        "x3": ((rows, 2, 128, 768), BF),
        "x3r": ((rows, 2, 128, 768), BF),
        "dfi": ((rows, 256, 768), F32),
        "dal": ((rows, 2, 2, 128, 768), BF),
        "dctx": ((512, 256), BF),
        "dsc": ((3, 512, 512), BF),
        "dmx": ((rows, 512, 640), BF),
        "p4": ((rows, 2, 2, 128, 768), BF),
        "p4r": ((rows, 2, 128, 768), BF),
        "x4": ((2, 128, 768), BF),
        "x4r": ((2, 128, 768), BF),
        "vs": ((8, 768), F32),
        "vm": ((8, 768), F32),
    }
    if fused:
        plan["vy"] = ((8, 768), F32)
        plan["vt"] = ((8, 768), F32)
        plan["vz"] = ((half - 1, 8, 768), F32)
        share = 768 // (2 * half)
        for name, width in PIECES:
            plan["g_" + name] = ((half, 2, share, width), BF)
            plan["a_" + name] = ((half, share, width), BF)
            plan["s_" + name] = ((half - 1, share, width), BF)
            plan["b_" + name] = ((half - 1, share, width), BF)
            plan["t_" + name] = ((share, width), F32)
    return plan


LOCAL_COPIES = 24
REMOTE_COPIES = 128


def layer_kernel(rows, n_dp, fused, names, *refs):
    half = n_dp // 2
    tok_h, cot_h, wq_h, wo_h, wu_h, wd_h, seg, vec = refs[:8]
    n_out = 14 if fused else 4
    outs = refs[8 : 8 + n_out]
    buf = dict(zip(names, refs[8 + n_out : 8 + n_out + len(names)]))
    local_sem, send_sem, recv_sem = refs[8 + n_out + len(names) :]

    dp = lax.axis_index("dp")
    me = lax.axis_index("tensor")
    chip = me // 2
    core = lax.rem(me, 2)
    mate = (dp, chip * 2 + (1 - core))
    over = (dp, (1 - chip) * 2 + core)
    over_mate = (dp, (1 - chip) * 2 + (1 - core))
    zed = dp // 2
    why = lax.rem(dp, 2)

    def row_partner(step):
        return (lax.rem(zed + step, half) * 2 + why, me)

    counts = {"local": 0, "remote": 0}
    pending = []

    def fetch(src, dst):
        copy = pltpu.make_async_copy(src, dst, local_sem.at[counts["local"]])
        counts["local"] += 1
        copy.start()
        return copy

    def remote(src, dst, device):
        at = counts["remote"]
        counts["remote"] += 1
        return pltpu.make_async_remote_copy(
            src_ref=src,
            dst_ref=dst,
            send_sem=send_sem.at[at],
            recv_sem=recv_sem.at[at],
            device_id=device,
            device_id_type=MESH_ID,
        )

    def send(src, dst, device):
        copy = remote(src, dst, device)
        copy.start()
        pending.append(copy)
        return copy

    got_tok = [
        [fetch(tok_h.at[r, :, h], buf["tok"].at[r, h]) for h in range(2)] for r in range(rows)
    ]
    got_wq = [
        fetch(wq_h.at[:, 0:128], buf["wq"].at[0:3]),
        fetch(wq_h.at[0, 128:192], buf["wq"].at[3, 0:64]),
        fetch(wq_h.at[1, 128:192], buf["wq"].at[3, 64:128]),
        fetch(wq_h.at[2, 128:192], buf["wq"].at[4, 0:64]),
    ]
    got_wo = fetch(wo_h, buf["wo"].at[me, 0:192])
    got_wu = fetch(wu_h, buf["wu"])
    got_wd = fetch(wd_h, buf["wd"])
    got_cot = fetch(cot_h.at[:, core], buf["cot"])

    partners = [mate, over, over_mate]
    if fused:
        partners.append((zed * 2 + (1 - why), me))
        partners += [row_partner(step) for step in range(1, half)]
    barrier = pltpu.get_barrier_semaphore()
    for device in partners:
        pl.semaphore_signal(barrier, inc=1, device_id=device, device_id_type=MESH_ID)
    buf["wq"][4, 64:128] = jnp.zeros((64, 768), BF)
    buf["vs"][...] = jnp.zeros((8, 768), F32)
    pl.semaphore_wait(barrier, len(partners))

    got_wo.wait()
    own_wo = buf["wo"].at[me, 0:192]
    wo_mate = send(own_wo, own_wo, mate)
    wo_over = send(own_wo, own_wo, over)

    lane = lax.broadcasted_iota(jnp.int32, (256, 128), 1)
    low_half = lane < 64
    lane_row = lax.broadcasted_iota(jnp.int32, (512, 128), 1) < 64

    ctx_copies = []

    def attention(r):
        for copy in got_tok[r]:
            copy.wait()
        if r == 0:
            for copy in got_wq:
                copy.wait()
        mixed = dot(
            buf["tok"][r].reshape(512, 768), buf["wq"][...].reshape(640, 768), 1, 1
        ) + vec[0:1, 0:640]
        q_low = mixed[:, 0:128].astype(BF).astype(F32) * SCALE
        buf["mix"][r, :, 0:128] = q_low.astype(BF)
        buf["mix"][r, :, 128:384] = mixed[:, 128:384].astype(BF)
        tail = mixed[:, 384:512].astype(BF).astype(F32)
        buf["mix"][r, :, 384:512] = jnp.where(lane_row, tail * SCALE, tail).astype(BF)
        buf["mix"][r, :, 512:640] = mixed[:, 512:640].astype(BF)

        ids = seg[r : r + 1, :].astype(F32)
        ids = jnp.concatenate(
            [ids[:, 0:128], ids[:, 256:384], ids[:, 128:256], ids[:, 384:512]], axis=1
        )
        column = jnp.broadcast_to(ids, (128, 512)).T
        buf["bias"][...] = jnp.where(column[:, 0:1] == ids, 0.0, -1e30)

        k_a = buf["mix"][r, :, 128:256]
        v_a = buf["mix"][r, :, 256:384]
        k_b = pltpu.roll(buf["mix"][r, :, 384:512].astype(F32), 64, 1).astype(BF)
        v_b = buf["mix"][r, :, 512:640]
        v_b_up = pltpu.roll(v_b.astype(F32), 64, 1).astype(BF)
        for h in range(2):
            at = pl.ds(h * 256, 256)
            q_a = buf["mix"][r, at, 0:128]
            q_b = buf["mix"][r, at, 384:512]
            zero = jnp.zeros_like(q_a)
            parts = []
            for head in range(3):
                query = jnp.where(low_half, q_b if head == 2 else q_a, zero)
                if head == 1:
                    query = jnp.where(low_half, zero, q_a)
                scores = dot(query, k_b if head == 2 else k_a, 1, 1) + buf["bias"][at, :]
                top = jnp.max(scores, axis=-1, keepdims=True)
                expo = jnp.exp(scores - top)
                probs = expo * (1.0 / jnp.sum(expo, axis=-1, keepdims=True))
                buf["prob"][r, head, at, :] = probs
                value = v_a if head < 2 else (v_b if h == 0 else v_b_up)
                parts.append(dot(probs.astype(BF), value, 1, 0))
            buf["ctx"][r, at, 0:128] = jnp.where(low_half, parts[0], parts[1]).astype(BF)
            buf["ctx"][r, at, 128:256] = parts[2].astype(BF)
        for part in range(2):
            here = [
                buf["ctx"][r, h * 256 + part * 128 : h * 256 + part * 128 + 128, :]
                for h in range(2)
            ]
            buf["cs"][r, part, 0:128] = here[0][:, 0:128]
            buf["cs"][r, part, 128:256] = here[1][:, 0:128]
            buf["cs"][r, part, 256:384] = jnp.where(
                lane[0:128] < 64, here[0][:, 128:256], here[1][:, 128:256]
            )
        ctx_copies.append(
            [
                send(buf["cs"].at[r, core], buf["cr"].at[r, me], over),
                send(buf["cs"].at[r, 1 - core], buf["cr"].at[r, me], over_mate),
                send(buf["cs"].at[r, 1 - core], buf["cr"].at[r, me], mate),
            ]
        )
        buf["cr"][r, me] = buf["cs"][r, core]

    flow_copies = {}

    def first_norm(r):
        for copy in ctx_copies[r]:
            copy.wait_recv()
        total = None
        for group in range(4):
            packed = buf["cr"][r, group, 256:384]
            zero = jnp.zeros_like(packed)
            keep = lane[0:128] < 64
            left = jnp.concatenate(
                [
                    buf["cr"][r, group, 0:256],
                    jnp.concatenate(
                        [jnp.where(keep, packed, zero), jnp.where(keep, zero, packed)], axis=0
                    ),
                ],
                axis=1,
            )
            term = dot(left, buf["wo"][group], 1, 0).astype(BF).astype(F32)
            total = term if total is None else total + term
        first_in = buf["tok"][r, :, core].reshape(256, 768).astype(F32) + total + vec[1:2, :]
        center = first_in - mean_of(first_in)
        scale = lax.rsqrt(mean_of(center * center) + EPS)
        unit = center * scale
        buf["n1"][r] = unit
        buf["r1"][r] = scale
        first_out = unit * vec[2:3, :] + vec[3:4, :]
        buf["fo"][r] = first_out
        first_low = first_out.astype(BF)
        for h in range(2):
            buf["flow"][r, h, core] = first_low[h * 128 : h * 128 + 128]
            own = buf["flow"].at[r, h, core]
            flow_copies[r, h] = send(own, own, mate)

    pair_copies = {}
    cross_copies = {}

    def ffn_forward(r, h):
        flow_copies[r, h].wait_recv()
        rows_in = buf["flow"][r, h].reshape(256, 768)
        for part in range(3):
            at = pl.ds(part * 256, 256)
            hidden = dot(rows_in, buf["wu"][:, at], 1, 0) + vec[4:5, at]
            phi = 0.5 * (1.0 + lax.erf(hidden * 0.7071067811865476))
            buf["act"][r, h, :, at] = (hidden * phi).astype(BF)
            buf["gp"][r, h, :, at] = (
                phi + hidden * jnp.exp(-0.5 * hidden * hidden) * 0.3989422804014327
            )
        terms = dot(buf["act"][r, h], buf["wd"][...], 1, 0).astype(BF)
        buf["p2"][r, h] = terms.reshape(2, 128, 768)
        pair_copies[2, r, h] = send(buf["p2"].at[r, h, 1 - core], buf["p2r"].at[r, h], mate)

    def exchange(stage, r, h):
        pair_copies[stage, r, h].wait_recv()
        own = buf["p%d" % stage][r, h, core].astype(F32)
        other = buf["p%dr" % stage][r, h].astype(F32)
        buf["x%d" % stage][r, h] = (own + other).astype(BF)
        cross_copies[stage, r, h] = send(
            buf["x%d" % stage].at[r, h], buf["x%dr" % stage].at[r, h], over
        )

    def crossed(stage, r, h):
        cross_copies[stage, r, h].wait_recv()
        return buf["x%d" % stage][r, h].astype(F32) + buf["x%dr" % stage][r, h].astype(F32)

    dsl_copies = {}

    def second_norm(r, h):
        total = crossed(2, r, h)
        at = pl.ds(h * 128, 128)
        second_in = buf["fo"][r, at, :] + total + vec[5:6, :]
        center = second_in - mean_of(second_in)
        scale = lax.rsqrt(mean_of(center * center) + EPS)
        unit = center * scale

        @pl.when(chip == r)
        def _():
            layer = unit * vec[6:7, :] + vec[7:8, :]
            outs[0][at, :] = layer.astype(BF)

        grad = buf["cot"][r, h].astype(F32)
        scaled = grad * vec[6:7, :]
        d_second = scale * (scaled - mean_of(scaled) - unit * mean_of(scaled * unit))
        buf["ds"][r, at, :] = d_second
        buf["dsl"][r, h, core] = d_second.astype(BF)
        own = buf["dsl"].at[r, h, core]
        dsl_copies[r, h] = send(own, own, mate)
        buf["vs"][0:1, :] += row_sum(grad * unit)
        buf["vs"][1:2, :] += row_sum(grad)
        buf["vs"][2:3, :] += row_sum(d_second)

    def ffn_backward(r, h):
        dsl_copies[r, h].wait_recv()
        rows_in = buf["dsl"][r, h].reshape(256, 768)
        for part in range(3):
            at = pl.ds(part * 256, 256)
            d_hidden = dot(rows_in, buf["wd"][at, :], 1, 1) * buf["gp"][r, h, :, at]
            buf["vs"][6:7, at] += row_sum(d_hidden)
            buf["dhl"][r, h, :, at] = d_hidden.astype(BF)
        terms = dot(buf["dhl"][r, h], buf["wu"][...], 1, 1).astype(BF)
        buf["p3"][r, h] = terms.reshape(2, 128, 768)
        pair_copies[3, r, h] = send(buf["p3"].at[r, h, 1 - core], buf["p3r"].at[r, h], mate)

    dal_copies = {}

    def first_norm_back(r, h):
        total = crossed(3, r, h)
        at = pl.ds(h * 128, 128)
        d_first = buf["ds"][r, at, :] + total
        unit = buf["n1"][r, at, :]
        scaled = d_first * vec[2:3, :]
        d_in = buf["r1"][r, at, :] * (scaled - mean_of(scaled) - unit * mean_of(scaled * unit))
        buf["dfi"][r, at, :] = d_in
        buf["dal"][r, h, core] = d_in.astype(BF)
        own = buf["dal"].at[r, h, core]
        dal_copies[r, h] = send(own, own, mate)
        buf["vs"][3:4, :] += row_sum(d_first * unit)
        buf["vs"][4:5, :] += row_sum(d_first)
        buf["vs"][5:6, :] += row_sum(d_in)

    out_parts = []

    def attention_back(r):
        for h in range(2):
            dal_copies[r, h].wait_recv()
        buf["dctx"][...] = dot(
            buf["dal"][r].reshape(512, 768), buf["wo"][me], 1, 1
        ).astype(BF)
        q_a = buf["mix"][r, :, 0:128]
        k_a = buf["mix"][r, :, 128:256]
        v_a = buf["mix"][r, :, 256:384]
        qk_b = buf["mix"][r, :, 384:512]
        qk_roll = pltpu.roll(qk_b.astype(F32), 64, 1).astype(BF)
        v_b = buf["mix"][r, :, 512:640]
        d_q, d_k, d_v = [], [], []
        for head in range(3):
            tile = pl.ds((head // 2) * 128, 128)
            value = v_a if head < 2 else v_b
            for h in range(2):
                at = pl.ds(h * 256, 256)
                d_rows = buf["dctx"][at, tile]
                if head == 0:
                    d_rows = jnp.where(low_half, d_rows, jnp.zeros_like(d_rows))
                if head == 1:
                    d_rows = jnp.where(low_half, jnp.zeros_like(d_rows), d_rows)
                probs = buf["prob"][r, head, at, :]
                weighted = probs * dot(d_rows, value, 1, 1)
                inner = jnp.sum(weighted, axis=-1, keepdims=True)
                buf["dsc"][head, at, :] = (weighted - probs * inner).astype(BF)
            d_scores = buf["dsc"][head]
            d_q.append(dot(d_scores, k_a if head < 2 else qk_roll, 1, 0))
            d_k.append(dot(d_scores, q_a if head < 2 else qk_roll, 0, 0))
            d_v.append(dot(buf["prob"][r, head].astype(BF), buf["dctx"][:, tile], 0, 0))
        tiles = [
            jnp.where(lane_row, d_q[0], d_q[1]) * SCALE,
            jnp.where(lane_row, d_k[0], d_k[1]),
            jnp.where(lane_row, d_v[0], d_v[1]),
            jnp.where(lane_row, d_q[2] * SCALE, d_k[2]),
            jnp.where(lane_row, d_v[2], 0.0),
        ]
        for at, tile in enumerate(tiles):
            lanes = pl.ds(at * 128, 128)
            buf["dmx"][r, :, lanes] = tile.astype(BF)
            if at != 1:
                buf["vs"][7:8, lanes] += row_sum(tile)

    tok_copies = []

    def token_terms(r, h):
        terms = dot(
            buf["dmx"][r, h * 256 : h * 256 + 256, :], buf["wq"][...].reshape(640, 768), 1, 0
        )
        buf["p4"][r, h] = terms.astype(BF).reshape(2, 128, 768)
        pair_copies[4, r, h] = send(buf["p4"].at[r, h, 1 - core], buf["p4r"].at[r, h], mate)

    cross4 = [remote(buf["x4"].at[h], buf["x4r"].at[h], over) for h in range(2)]

    def token_cross(r, h):
        pair_copies[4, r, h].wait_recv()

        @pl.when(chip != r)
        def _():
            own = buf["p4"][r, h, core].astype(F32)
            other = buf["p4r"][r, h].astype(F32)
            buf["x4"][h] = (own + other).astype(BF)
            cross4[h].start()

    def token_finish(h):
        cross4[h].wait_recv()
        own = buf["p4"][chip, h, core].astype(F32)
        other = buf["p4r"][chip, h].astype(F32)
        pair = (own + other).astype(BF).astype(F32)
        total = pair + buf["x4r"][h].astype(F32)
        result = buf["dfi"][chip, pl.ds(h * 128, 128), :] + total
        outs[1][h * 128 : h * 128 + 128, :] = result.astype(BF)

    first_copies = {}
    second_copies = {}
    starts = {}
    column = 0
    for name, width in PIECES:
        starts[name] = column
        column += width

    def reduce_start(name, grad):
        width = dict(PIECES)[name]
        if not fused:
            outs[2][:, starts[name] : starts[name] + width] = grad
            return
        stage = buf["g_" + name]
        stage[...] = grad.astype(BF).reshape(stage.shape)
        first_copies[name] = send(
            stage.at[:, 1 - why], buf["a_" + name], (zed * 2 + (1 - why), me)
        )

    def reduce_middle(name):
        if not fused:
            return
        first_copies[name].wait_recv()
        stage, came = buf["g_" + name], buf["a_" + name]
        copies = []
        for step in range(1, half):
            target = lax.rem(zed + step, half)
            both = stage[target, why].astype(F32) + came[target].astype(F32)
            buf["s_" + name][step - 1] = both.astype(BF)
            copies.append(
                send(
                    buf["s_" + name].at[step - 1],
                    buf["b_" + name].at[step - 1],
                    row_partner(step),
                )
            )
        second_copies[name] = copies
        buf["t_" + name][...] = stage[zed, why].astype(F32) + came[zed].astype(F32)

    def reduce_finish(name):
        if not fused:
            return
        total = buf["t_" + name][...]
        for step, copy in enumerate(second_copies[name]):
            copy.wait_recv()
            total = total + buf["b_" + name][step].astype(F32)
        if name[0] == "d":
            outs[10][:, starts[name] : starts[name] + 256] = total
        elif name[0] == "u":
            at = starts[name] - starts["u0"]
            outs[8][:, at : at + 256] = total
        elif name == "o":
            outs[4][0:128, :] = total.T
        elif name == "q":
            for kind in range(3):
                outs[2][kind * 192 : kind * 192 + 128, :] = total[
                    :, kind * 128 : kind * 128 + 128
                ].T
        else:
            for at in range(4):
                flipped = total[:, (at // 2) * 128 : (at // 2) * 128 + 128].T
                piece = flipped[(at % 2) * 64 : (at % 2) * 64 + 64]
                if at < 3:
                    outs[2][at * 192 + 128 : at * 192 + 192, :] = piece
                else:
                    outs[4][128:192, :] = piece

    def down_grad(part):
        at = pl.ds(part * 256, 256)
        return dot(
            buf["dsl"][...].reshape(rows * 512, 768),
            buf["act"][:, :, :, at].reshape(rows * 512, 256),
            0,
            0,
        )

    def up_grad(part):
        at = pl.ds(part * 256, 256)
        return dot(
            buf["flow"][...].reshape(rows * 512, 768),
            buf["dhl"][:, :, :, at].reshape(rows * 512, 256),
            0,
            0,
        )

    def out_grad_first():
        return dot(
            buf["dal"][...].reshape(rows * 512, 768),
            buf["ctx"][:, :, 0:128].reshape(rows * 512, 128),
            0,
            0,
        )

    def out_grad_second():
        sides = []
        for h in range(2):
            sides.append(
                dot(
                    buf["dal"][:, h].reshape(rows * 256, 768),
                    buf["ctx"][:, h * 256 : h * 256 + 256, 128:256].reshape(rows * 256, 128),
                    0,
                    0,
                )
            )
        return pltpu.roll(sides[0], 64, 1) + sides[1]

    def qkv_grad(low, high):
        return dot(
            buf["tok"][...].reshape(rows * 512, 768),
            buf["dmx"][:, :, low:high].reshape(rows * 512, high - low),
            0,
            0,
        )

    attention(0)
    wo_over.wait_recv()
    theirs = buf["wo"].at[(1 - chip) * 2 + core, 0:192]
    wo_far = send(theirs, theirs, mate)
    attention(1)
    wo_mate.wait_recv()
    wo_far.wait_recv()
    for group in range(4):
        buf["wo"][group, 192:256] = buf["wo"][group, 128:192]
    first_norm(0)
    got_wu.wait()
    got_wd.wait()
    got_cot.wait()
    ffn_forward(0, 0)
    ffn_forward(0, 1)
    exchange(2, 0, 0)
    first_norm(1)
    exchange(2, 0, 1)
    ffn_forward(1, 0)
    ffn_forward(1, 1)
    exchange(2, 1, 0)
    second_norm(0, 0)
    exchange(2, 1, 1)
    ffn_backward(0, 0)
    second_norm(0, 1)
    exchange(3, 0, 0)
    ffn_backward(0, 1)
    second_norm(1, 0)
    exchange(3, 0, 1)
    ffn_backward(1, 0)
    second_norm(1, 1)
    exchange(3, 1, 0)
    ffn_backward(1, 1)
    reduce_start("d0", down_grad(0))
    exchange(3, 1, 1)
    reduce_start("u0", up_grad(0))
    reduce_start("d1", down_grad(1))
    first_norm_back(0, 0)
    reduce_start("u1", up_grad(1))
    reduce_start("d2", down_grad(2))
    reduce_middle("d0")
    first_norm_back(0, 1)
    reduce_start("u2", up_grad(2))
    reduce_middle("u0")
    attention_back(0)
    reduce_middle("d1")
    token_terms(0, 0)
    token_terms(0, 1)
    token_cross(0, 0)
    first_norm_back(1, 0)
    token_cross(0, 1)
    reduce_middle("u1")
    first_norm_back(1, 1)
    attention_back(1)
    token_terms(1, 0)
    token_terms(1, 1)
    reduce_start("o", out_grad_first())
    token_cross(1, 0)
    reduce_start("q", qkv_grad(0, 384))
    token_cross(1, 1)
    tail = qkv_grad(384, 640)
    merged = jnp.concatenate(
        [
            tail[:, 0:128],
            jnp.where(
                lax.broadcasted_iota(jnp.int32, (768, 128), 1) < 64,
                tail[:, 128:256],
                out_grad_second(),
            ),
        ],
        axis=1,
    )
    reduce_start("r", merged)

    vec_mate = send(buf["vs"], buf["vm"], mate)
    reduce_middle("d2")
    reduce_middle("u2")
    vec_mate.wait_recv()
    shared = lax.broadcasted_iota(jnp.int32, (8, 768), 0) < 6
    small = buf["vs"][...] + jnp.where(shared, buf["vm"][...], 0.0)
    if fused:
        buf["vt"][...] = small
        vec_row = send(buf["vt"], buf["vy"], (zed * 2 + (1 - why), me))
    else:
        outs[3][...] = small
    for name in ("d0", "u0", "d1", "u1"):
        reduce_finish(name)
    reduce_middle("o")
    reduce_middle("q")
    reduce_middle("r")
    if fused:
        vec_row.wait_recv()
        vec_row.wait_send()
        pending[:] = [copy for copy in pending if copy is not vec_row]
        small = small + buf["vy"][...]
        buf["vt"][...] = small
        vec_far = [send(buf["vt"], buf["vz"].at[s - 1], row_partner(s)) for s in range(1, half)]
    token_finish(0)
    token_finish(1)
    for name in ("d2", "u2", "o"):
        reduce_finish(name)
    if fused:
        for step, copy in enumerate(vec_far):
            copy.wait_recv()
            small = small + buf["vz"][step]
        share = 768 // n_dp
        turned = pltpu.roll(small, 768 - dp * share, 1)
        for row, at in ((5, 5), (3, 6), (4, 7), (2, 11), (0, 12), (1, 13)):
            outs[at][...] = turned[row : row + 1, 0:share]
        wide = HEAD // n_dp
        lanes = lax.broadcasted_iota(jnp.int32, (8, 768), 1)
        depth = lax.broadcasted_iota(jnp.int32, (8, 768), 0)
        spread = jnp.where(lax.rem(lanes, HEAD) == depth + dp * wide, small[6:7, :], 0.0)
        group = lax.broadcasted_iota(jnp.int32, (768, 128), 0) // HEAD
        pick = (group == lax.broadcasted_iota(jnp.int32, (768, 128), 1)).astype(F32)
        outs[9][...] = jnp.dot(spread, pick, precision=lax.Precision.HIGHEST)[0:wide, 0:12]
        group = lanes // HEAD
        where = jnp.where(
            depth < 4,
            lax.rem(depth, 2) * 4 + depth // 2,
            jnp.where(depth == 4, 6, 8),
        )
        spread = jnp.where((group == where) & (depth < 6), small[7:8, :], 0.0)
        inside = lax.rem(lax.broadcasted_iota(jnp.int32, (768, 128), 0), HEAD)
        pick = (inside == lax.broadcasted_iota(jnp.int32, (768, 128), 1) + dp * wide).astype(F32)
        heads = jnp.dot(spread, pick, precision=lax.Precision.HIGHEST)
        for head in range(3):
            outs[3][head] = heads[head * 2 : head * 2 + 2, 0:wide]
    reduce_finish("q")
    reduce_finish("r")
    for copy in pending + cross4:
        copy.wait_send()


def body(
    tokens,
    segment_ids,
    qkv_weight,
    qkv_bias,
    output_weight,
    output_bias,
    first_gain,
    first_shift,
    up_weight,
    up_bias,
    down_weight,
    down_bias,
    second_gain,
    second_shift,
    cotangent,
):
    rows = tokens.shape[0] // SEQ
    n_dp = lax.axis_size("dp")
    share = 768 // n_dp
    fused = share % 16 == 0 and n_dp % 2 == 0
    split = (rows, 2, 2, 128, 768)
    pad = jnp.zeros((64,), BF)
    bias_q = qkv_bias[0].reshape(192)
    bias_v = qkv_bias[1].reshape(192)
    vectors = jnp.stack(
        [
            jnp.concatenate(
                [bias_q[:128], pad, pad, bias_v[:128], bias_q[128:], pad, bias_v[128:], pad, pad, pad]
            ),
            output_bias,
            first_gain,
            first_shift,
            up_bias.reshape(768),
            down_bias,
            second_gain,
            second_shift,
        ]
    ).astype(F32)
    plan = scratch_plan(rows, n_dp // 2, fused)
    shape = jax.ShapeDtypeStruct
    outs = [shape((256, 768), BF), shape((256, 768), BF)]
    if fused:
        wide = HEAD // n_dp
        vector = shape((1, share), F32)
        outs += [
            shape((576, share), F32),
            shape((3, 2, wide), F32),
            shape((192, share), F32),
            vector,
            vector,
            vector,
            shape((share, 768), F32),
            shape((wide, 12), F32),
            shape((share, 768), F32),
            vector,
            vector,
            vector,
        ]
    else:
        outs += [shape((768, 2304), F32), shape((8, 768), F32)]
    whole = pl.BlockSpec(memory_space=pltpu.VMEM)
    anywhere = pl.BlockSpec(memory_space=pl.ANY)

    def kernel(*refs):
        layer_kernel(rows, n_dp, fused, list(plan), *refs)

    got = pl.pallas_call(
        kernel,
        out_shape=outs,
        in_specs=[anywhere] * 6 + [whole] * 2,
        out_specs=[whole] * len(outs),
        scratch_shapes=[pltpu.VMEM(dims, kind) for dims, kind in plan.values()]
        + [
            pltpu.SemaphoreType.DMA((LOCAL_COPIES,)),
            pltpu.SemaphoreType.DMA((REMOTE_COPIES,)),
            pltpu.SemaphoreType.DMA((REMOTE_COPIES,)),
        ],
        compiler_params=pltpu.CompilerParams(
            collective_id=0, has_side_effects=True, vmem_limit_bytes=62 * 1024 * 1024
        ),
    )(
        tokens.reshape(split),
        cotangent.reshape(split),
        qkv_weight.transpose(1, 2, 3, 0).reshape(3, 192, 768),
        output_weight.reshape(192, 768),
        up_weight,
        down_weight,
        segment_ids,
        vectors,
    )
    if not fused:
        got = finish_plain(n_dp, *got)
    return (
        got[0],
        got[1],
        got[2].reshape(3, 3, HEAD, share).transpose(3, 0, 1, 2),
        got[3].transpose(1, 0, 2),
        got[4].reshape(3, HEAD, share),
        got[5].reshape(share),
        got[6].reshape(share),
        got[7].reshape(share),
        got[8],
        got[9].T,
        got[10].T,
        got[11].reshape(share),
        got[12].reshape(share),
        got[13].reshape(share),
    )


def finish_plain(n_dp, layer, tokens_grad, grads, small):
    share = 768 // n_dp
    grads = lax.psum_scatter(grads, "dp", scatter_dimension=0, tiled=True)
    small = lax.psum(small, "dp")
    dp = lax.axis_index("dp")
    wide = HEAD // n_dp
    turned = lax.dynamic_slice_in_dim(small, dp * share, share, 1)
    up_bias = lax.dynamic_slice_in_dim(small[6].reshape(12, HEAD), dp * wide, wide, 1)
    row = small[7]
    sums = jnp.stack(
        [row[0:64], row[256:320], row[64:128], row[320:384], row[384:448], row[512:576]]
    )
    sums = lax.dynamic_slice_in_dim(sums, dp * wide, wide, 1)
    down, up = grads[:, 0:768], grads[:, 768:1536]
    out_a, main, tail = grads[:, 1536:1664], grads[:, 1664:2048], grads[:, 2048:2304]
    qkv = jnp.concatenate(
        [
            main[:, 0:128],
            tail[:, 0:64],
            main[:, 128:256],
            tail[:, 64:128],
            main[:, 256:384],
            tail[:, 128:192],
        ],
        axis=1,
    )
    out = jnp.concatenate([out_a, tail[:, 192:256]], axis=1)
    return [
        layer,
        tokens_grad,
        qkv.T,
        sums.reshape(3, 2, wide),
        out.T,
        turned[5],
        turned[3],
        turned[4],
        up,
        up_bias.T,
        down,
        turned[2],
        turned[0],
        turned[1],
    ]


def solution(mesh):
    placed = (
        P("dp", None),
        P("dp", None),
        P(None, None, "tensor", None),
        P(None, "tensor", None),
        P("tensor", None, None),
        P(),
        P(),
        P(),
        P(None, "tensor"),
        P("tensor", None),
        P("tensor", None),
        P(),
        P(),
        P(),
        P("dp", None),
    )
    return jax.shard_map(
        body,
        mesh=mesh,
        in_specs=placed,
        out_specs=(
            P(("dp", "tensor"), None),
            P(("dp", "tensor"), None),
            P("dp", None, "tensor", None),
            P(None, "tensor", "dp"),
            P("tensor", None, "dp"),
            P("dp"),
            P("dp"),
            P("dp"),
            P("dp", "tensor"),
            P("tensor", "dp"),
            P("tensor", "dp"),
            P("dp"),
            P("dp"),
            P("dp"),
        ),
        check_vma=False,
    )
```

time: 560 us -> 122 us (0.22)
  waiting for transfers between devices: 374 us -> 0 us
  Pallas kernels: 0 us -> 103 us
  matrix products: 58.2 us -> 0 us
  blocking collectives: 37.5 us -> 0 us
  other arithmetic: 33.5 us -> 0.61 us
  between operations: 16.9 us -> 0.75 us
  local copies, waits for them, and re-layouts: 33.3 us -> 17.4 us
    reduce_scatter x2 -> x0, waiting for transfers between devices: 143 us -> none  [the longest x1 72.3 us: body(): lax.psum_scatter(up_grad, 'dp', scatter_dimension=0, tiled=True)]
    psum x4 -> x0, waiting for transfers between devices: 126 us -> none  [the longest x1 43.5 us: body(): lax.psum(attn_terms.astype(jnp.bfloat16), 'tensor').astype(jnp.float32)]
    unnamed x10 -> x0, waiting for transfers between devices: 105 us -> none
    pallas_call x0 -> x1, Pallas kernels: none -> 103 us  [body(): pl.pallas_call(kernel, out_shape=outs, in_specs=[anywhere] * 6 + [whole]...]
    dot_general x18 -> x0, matrix products: 58.2 us -> none  [the longest x1 9.89 us: body(): jnp.dot(first_low, up_weight, preferred_element_type=jnp.float32)]
    unnamed x1 -> x0, blocking collectives: 37.5 us -> none
    reduce_sum x9 -> x0, other arithmetic: 21.7 us -> none  [the longest x3 8.95 us: normalize(): center = rows_in - jnp.mean(rows_in, axis=-1, keepdims=True)]
    unnamed x161 -> x38, local copies, waits for them, and re-layouts: 25.7 us -> 10.7 us
  transfers between devices with their start and end apart: 8 -> 0, of which waited for: 7 -> 0; matrix products, arithmetic and copies ran while one was open for 7% -> 0% of each run, Pallas kernels for 0% -> 0%
where the time goes in v1:
time: 122 us; the launch traced here: 121 us
  Pallas kernels  103 us (84%)
  local copies, waits for them, and re-layouts  17.4 us (14%)
    pallas_call x1, Pallas kernels, body(): pl.pallas_call(kernel, out_shape=outs, in_specs=[anywhere] * 6 + [whole]...  103 us
    unnamed x38, local copies, waits for them, and re-layouts  10.7 us
    another operation x9, local copies, waits for them, and re-layouts, body(): jnp.stack([jnp.concatenate([bias_q[:128], pad, pad, bias_v[:128], bias_q[...  4.94 us

profile of v1, /device:TPU:0, one launch (start us, length us, event | category | flops | bytes accessed | tf_op | source)
XLA Modules:
  0.0 121.3 jit_solution(9436009148423960136)
XLA Ops:
  0.6 0.7 slice_bitcast_fusion
  1.4 0.8 slice_reduce_fusion
  2.2 0.1 slice.33
  2.2 0.1 slice.31
  2.3 0.1 concatenate.11
  2.4 0.7 stack.25
  3.1 0.7 stack.26
  3.8 0.7 stack.27
  4.5 0.8 stack_reshape.3
  5.3 0.7 stack.28
  6.0 0.7 stack.29
  6.6 0.7 stack.30
  7.4 0.6 convert_element_type.3.refs_7_
  8.0 102.6 %shard_map.254 = (bf16[256,768]{1,0:T(8,128)(2,1)}, bf16[256,768]{1,0:T(8,128)(2,1)}, f32[576,96]{1,0:T(8,128)}, f32[3,2,8]{2,1,0:T(2,128)}, f32[192,96]{1,0:T(8...) custom-call(bf16[2,2,2,128,768]{4,3,2,1,0:T(8,128)(2,1)} %bitcast.23, ...), custom_call_target="tpu_custom_call" | custom-call | tf_op jit(solution)/shard_map/pallas_call | solution.py:766
  110.6 0.0 copy-start.2
  110.6 0.0 copy-start.5
  110.6 0.0 copy-start.3
  110.6 0.0 copy-start.11
  110.6 0.0 copy-start.10
  110.6 0.0 copy-start.9
  110.6 0.0 copy-start.1
  110.6 0.0 copy-start.4
  110.7 0.0 copy-start
  110.7 1.8 %copy.43 = bf16[256,768]{1,0:T(8,128)(2,1)} copy(bf16[256,768]{1,0:T(8,128)(2,1)} %get-tuple-element.60) | data formatting | bytes 786432
  112.5 1.8 %copy.44 = bf16[256,768]{1,0:T(8,128)(2,1)} copy(bf16[256,768]{1,0:T(8,128)(2,1)} %get-tuple-element.61) | data formatting | bytes 786432
  114.3 0.0 copy-done.2
  114.3 0.7 copy.45
  115.0 0.0 copy-done.5
  115.0 0.6 copy.46
  115.6 0.0 copy-done.3
  115.6 0.6 copy.47
  116.2 0.0 copy-done.11
  116.2 0.5 copy.48
  116.7 0.0 copy-done.10
  116.7 0.5 copy.49
  117.3 0.0 copy-done.9
  117.3 0.5 copy.50
  117.8 0.0 copy-done.1
  117.8 0.7 copy.51
  118.5 0.0 copy-done.4
  118.5 0.6 copy.52
  119.1 0.0 copy-done
  119.1 0.7 copy.53
  119.8 0.0 copy-done.8
  119.8 0.5 copy.54
  120.3 0.0 copy-done.7
  120.3 0.5 copy.55
  120.8 0.5 copy.56
  (9 shorter events, 0.1 us)
Async XLA Ops:
  110.6 3.7 %copy-start.2 = (f32[576,96]{1,0:T(8,128)S(1)}, f32[576,96]{1,0:T(8,128)}, u32[]{:S(2)}) copy-start(f32[576,96]{1,0:T(8,128)} %get-tuple-element.30) | copy-start | bytes 663556
  110.6 4.4 %copy-start.5 = (f32[3,2,8]{2,1,0:T(2,128)S(1)}, f32[3,2,8]{2,1,0:T(2,128)}, u32[]{:S(2)}) copy-start(f32[3,2,8]{2,1,0:T(2,128)} %get-tuple-element.31) | copy-start | bytes 580
  110.6 5.0 %copy-start.3 = (f32[192,96]{1,0:T(8,128)S(1)}, f32[192,96]{1,0:T(8,128)}, u32[]{:S(2)}) copy-start(f32[192,96]{1,0:T(8,128)} %get-tuple-element.32) | copy-start | bytes 221188
  110.6 5.6 %copy-start.11 = (f32[1,96]{1,0:T(1,128)S(1)}, f32[1,96]{1,0:T(1,128)}, u32[]{:S(2)}) copy-start(f32[1,96]{1,0:T(1,128)} %get-tuple-element.33) | copy-start | bytes 1156
  110.6 6.1 %copy-start.10 = (f32[1,96]{1,0:T(1,128)S(1)}, f32[1,96]{1,0:T(1,128)}, u32[]{:S(2)}) copy-start(f32[1,96]{1,0:T(1,128)} %get-tuple-element.34) | copy-start | bytes 1156
  110.6 6.6 %copy-start.9 = (f32[1,96]{1,0:T(1,128)S(1)}, f32[1,96]{1,0:T(1,128)}, u32[]{:S(2)}) copy-start(f32[1,96]{1,0:T(1,128)} %get-tuple-element.35) | copy-start | bytes 1156
  110.6 7.1 %copy-start.1 = (f32[96,768]{1,0:T(8,128)S(1)}, f32[96,768]{1,0:T(8,128)}, u32[]{:S(2)}) copy-start(f32[96,768]{1,0:T(8,128)} %get-tuple-element.68) | copy-start | bytes 884740
  110.6 7.8 %copy-start.4 = (f32[8,12]{1,0:T(8,128)S(1)}, f32[8,12]{1,0:T(8,128)}, u32[]{:S(2)}) copy-start(f32[8,12]{1,0:T(8,128)} %get-tuple-element.37) | copy-start | bytes 1156
  110.7 8.4 %copy-start = (f32[96,768]{1,0:T(8,128)S(1)}, f32[96,768]{1,0:T(8,128)}, u32[]{:S(2)}) copy-start(f32[96,768]{1,0:T(8,128)} %get-tuple-element.38) | copy-start | bytes 884740
  112.5 7.3 %copy-start.8 = (f32[1,96]{1,0:T(1,128)S(1)}, f32[1,96]{1,0:T(1,128)}, u32[]{:S(2)}) copy-start(f32[1,96]{1,0:T(1,128)} %get-tuple-element.39) | copy-start | bytes 1156
  112.5 7.8 %copy-start.7 = (f32[1,96]{1,0:T(1,128)S(1)}, f32[1,96]{1,0:T(1,128)}, u32[]{:S(2)}) copy-start(f32[1,96]{1,0:T(1,128)} %get-tuple-element.40) | copy-start | bytes 1156
  112.5 8.3 %copy-start.6 = (f32[1,96]{1,0:T(1,128)S(1)}, f32[1,96]{1,0:T(1,128)}, u32[]{:S(2)}) copy-start(f32[1,96]{1,0:T(1,128)} %get-tuple-element.41) | copy-start | bytes 1156

commit v2 on v1

--- a/solution.py
+++ b/solution.py
@@ -22,8 +22,10 @@
     ("u2", 256),
     ("o", 128),
     ("q", 384),
-    ("r", 256),
+    ("r", 128),
+    ("s", 128),
 )
+DEPTH_FIRST = ("d1", "u2")
 
 
 def dot(left, right, left_dim, right_dim):
@@ -40,8 +42,12 @@
     return jnp.sum(values, axis=0, keepdims=True)
 
 
-def scratch_plan(rows, half, fused):
+def scratch_plan(rows, share, fused, results):
     plan = {
+        "seg": ((rows, SEQ), jnp.int32),
+        "bqv": ((3, 2, HEAD), BF),
+        "bup": ((12, HEAD), BF),
+        "vec": ((8, 768), F32),
         "tok": ((rows, 2, 2, 128, 768), BF),
         "cot": ((rows, 2, 128, 768), BF),
         "wq": ((5, 128, 768), BF),
@@ -49,11 +55,12 @@
         "wu": ((768, 768), BF),
         "wd": ((768, 768), BF),
         "mix": ((rows, 512, 640), BF),
-        "bias": ((512, 512), F32),
+        "bias": ((rows, 512, 512), F32),
+        "mixr": ((rows, 512, 128), BF),
         "prob": ((rows, 3, 512, 512), F32),
         "ctx": ((rows, 512, 256), BF),
-        "cs": ((rows, 2, 384, 128), BF),
-        "cr": ((rows, 4, 384, 128), BF),
+        "cs": ((rows, 2, 2, 192, 128), BF),
+        "cr": ((rows, 2, 4, 192, 128), BF),
         "n1": ((rows, 256, 768), F32),
         "r1": ((rows, 256, 1), F32),
         "fo": ((rows, 256, 768), F32),
@@ -83,31 +90,37 @@
         "vs": ((8, 768), F32),
         "vm": ((8, 768), F32),
     }
+    for at in range(6):
+        plan["e%d" % at] = ((6, 128), BF)
+    for at, result in enumerate(results):
+        plan["y%d" % at] = (result.shape, result.dtype)
     if fused:
-        plan["vy"] = ((8, 768), F32)
-        plan["vt"] = ((8, 768), F32)
-        plan["vz"] = ((half - 1, 8, 768), F32)
-        share = 768 // (2 * half)
+        for name in ("vt", "vy", "vu", "vz", "vw", "vx"):
+            plan[name] = ((8, 768), F32)
         for name, width in PIECES:
-            plan["g_" + name] = ((half, 2, share, width), BF)
-            plan["a_" + name] = ((half, share, width), BF)
-            plan["s_" + name] = ((half - 1, share, width), BF)
-            plan["b_" + name] = ((half - 1, share, width), BF)
-            plan["t_" + name] = ((share, width), F32)
+            plan["g_" + name] = ((2, 2, 2, share, width), BF)
+            plan["a_" + name] = ((2, 2, share, width), BF)
+            plan["s_" + name] = ((2, share, width), BF)
+            plan["b_" + name] = ((2, share, width), BF)
+            plan["v_" + name] = ((share, width), BF)
+            plan["c_" + name] = ((share, width), BF)
     return plan
 
 
-LOCAL_COPIES = 24
+INPUTS = 15
+LOCAL_COPIES = 40
 REMOTE_COPIES = 128
 
 
 def layer_kernel(rows, n_dp, fused, names, *refs):
-    half = n_dp // 2
-    tok_h, cot_h, wq_h, wo_h, wu_h, wd_h, seg, vec = refs[:8]
+    tok_h, cot_h, wq_h, wo_h, wu_h, wd_h, seg_h = refs[:7]
+    small_h = refs[7:INPUTS]
     n_out = 14 if fused else 4
-    outs = refs[8 : 8 + n_out]
-    buf = dict(zip(names, refs[8 + n_out : 8 + n_out + len(names)]))
-    local_sem, send_sem, recv_sem = refs[8 + n_out + len(names) :]
+    results = refs[INPUTS : INPUTS + n_out]
+    buf = dict(zip(names, refs[INPUTS + n_out : INPUTS + n_out + len(names)]))
+    outs = [buf["y%d" % at] for at in range(n_out)]
+    seg, vec = buf["seg"], buf["vec"]
+    local_sem, send_sem, recv_sem = refs[INPUTS + n_out + len(names) :]
 
     dp = lax.axis_index("dp")
     me = lax.axis_index("tensor")
@@ -116,14 +129,16 @@
     mate = (dp, chip * 2 + (1 - core))
     over = (dp, (1 - chip) * 2 + core)
     over_mate = (dp, (1 - chip) * 2 + (1 - core))
-    zed = dp // 2
     why = lax.rem(dp, 2)
-
-    def row_partner(step):
-        return (lax.rem(zed + step, half) * 2 + why, me)
+    near = lax.rem(dp // 2, 2)
+    far = dp // 4
+    side = (dp + 1 - 2 * why, me)
+    next_near = (dp + 2 - 4 * near, me)
+    next_far = (dp + 4 - 8 * far, me)
 
     counts = {"local": 0, "remote": 0}
     pending = []
+    stored = []
 
     def fetch(src, dst):
         copy = pltpu.make_async_copy(src, dst, local_sem.at[counts["local"]])
@@ -143,12 +158,34 @@
             device_id_type=MESH_ID,
         )
 
+    arrived = []
+
+    def once(copy):
+        new = not any(copy is other for other in arrived)
+        if new:
+            arrived.append(copy)
+        return new
+
+    def arrive(copy):
+        if once(copy):
+            copy.wait_recv()
+
+    def loaded(copy):
+        if once(copy):
+            copy.wait()
+
     def send(src, dst, device):
         copy = remote(src, dst, device)
         copy.start()
         pending.append(copy)
         return copy
 
+    partners = [mate, over, over_mate]
+    if fused:
+        partners += [side, next_near, next_far]
+    barrier = pltpu.get_barrier_semaphore()
+    for device in partners:
+        pl.semaphore_signal(barrier, inc=1, device_id=device, device_id_type=MESH_ID)
     got_tok = [
         [fetch(tok_h.at[r, :, h], buf["tok"].at[r, h]) for h in range(2)] for r in range(rows)
     ]
@@ -158,39 +195,51 @@
         fetch(wq_h.at[1, 128:192], buf["wq"].at[3, 64:128]),
         fetch(wq_h.at[2, 128:192], buf["wq"].at[4, 0:64]),
     ]
+    got_small = [fetch(seg_h, buf["seg"]), fetch(small_h[0], buf["bqv"])]
+    got_small.append(fetch(small_h[1], buf["bup"]))
+    got_small += [fetch(small_h[2 + at], buf["e%d" % at]) for at in range(6)]
     got_wo = fetch(wo_h, buf["wo"].at[me, 0:192])
     got_wu = fetch(wu_h, buf["wu"])
     got_wd = fetch(wd_h, buf["wd"])
     got_cot = fetch(cot_h.at[:, core], buf["cot"])
 
-    partners = [mate, over, over_mate]
-    if fused:
-        partners.append((zed * 2 + (1 - why), me))
-        partners += [row_partner(step) for step in range(1, half)]
-    barrier = pltpu.get_barrier_semaphore()
-    for device in partners:
-        pl.semaphore_signal(barrier, inc=1, device_id=device, device_id_type=MESH_ID)
     buf["wq"][4, 64:128] = jnp.zeros((64, 768), BF)
     buf["vs"][...] = jnp.zeros((8, 768), F32)
-    pl.semaphore_wait(barrier, len(partners))
-
-    got_wo.wait()
-    own_wo = buf["wo"].at[me, 0:192]
-    wo_mate = send(own_wo, own_wo, mate)
-    wo_over = send(own_wo, own_wo, over)
+    for copy in got_small:
+        copy.wait()
+    bias = [[buf["bqv"][head, kind : kind + 1, :].astype(F32) for kind in range(2)] for head in range(3)]
+    none = jnp.zeros((1, HEAD), F32)
+    none2 = jnp.zeros((1, 128), F32)
+    for at, pair in enumerate(
+        (
+            (bias[0][0], bias[1][0]),
+            (none, none),
+            (bias[0][1], bias[1][1]),
+            (bias[2][0], none),
+            (bias[2][1], none),
+        )
+    ):
+        vec[0:1, at * 128 : at * 128 + 128] = jnp.concatenate(pair, axis=1)
+    vec[0:1, 640:768] = none2
+    for at in range(6):
+        pair = buf["bup"][2 * at : 2 * at + 2, :].astype(F32)
+        vec[4:5, at * 128 : at * 128 + 128] = jnp.concatenate([pair[0:1], pair[1:2]], axis=1)
+    for at, row in enumerate((1, 2, 3, 5, 6, 7)):
+        short = buf["e%d" % at][...].astype(F32)
+        for part in range(6):
+            vec[row : row + 1, part * 128 : part * 128 + 128] = short[part : part + 1]
 
     lane = lax.broadcasted_iota(jnp.int32, (256, 128), 1)
     low_half = lane < 64
     lane_row = lax.broadcasted_iota(jnp.int32, (512, 128), 1) < 64
 
-    ctx_copies = []
-
-    def attention(r):
+    ctx_copies = {}
+
+    def project(r):
         for copy in got_tok[r]:
             copy.wait()
-        if r == 0:
-            for copy in got_wq:
-                copy.wait()
+        for copy in got_wq:
+            loaded(copy)
         mixed = dot(
             buf["tok"][r].reshape(512, 768), buf["wq"][...].reshape(640, 768), 1, 1
         ) + vec[0:1, 0:640]
@@ -198,7 +247,9 @@
         buf["mix"][r, :, 0:128] = q_low.astype(BF)
         buf["mix"][r, :, 128:384] = mixed[:, 128:384].astype(BF)
         tail = mixed[:, 384:512].astype(BF).astype(F32)
-        buf["mix"][r, :, 384:512] = jnp.where(lane_row, tail * SCALE, tail).astype(BF)
+        tail = jnp.where(lane_row, tail * SCALE, tail)
+        buf["mix"][r, :, 384:512] = tail.astype(BF)
+        buf["mixr"][r] = pltpu.roll(tail, 64, 1).astype(BF)
         buf["mix"][r, :, 512:640] = mixed[:, 512:640].astype(BF)
 
         ids = seg[r : r + 1, :].astype(F32)
@@ -206,64 +257,79 @@
             [ids[:, 0:128], ids[:, 256:384], ids[:, 128:256], ids[:, 384:512]], axis=1
         )
         column = jnp.broadcast_to(ids, (128, 512)).T
-        buf["bias"][...] = jnp.where(column[:, 0:1] == ids, 0.0, -1e30)
-
-        k_a = buf["mix"][r, :, 128:256]
-        v_a = buf["mix"][r, :, 256:384]
-        k_b = pltpu.roll(buf["mix"][r, :, 384:512].astype(F32), 64, 1).astype(BF)
-        v_b = buf["mix"][r, :, 512:640]
-        v_b_up = pltpu.roll(v_b.astype(F32), 64, 1).astype(BF)
-        for h in range(2):
-            at = pl.ds(h * 256, 256)
-            q_a = buf["mix"][r, at, 0:128]
-            q_b = buf["mix"][r, at, 384:512]
-            zero = jnp.zeros_like(q_a)
-            parts = []
-            for head in range(3):
+        buf["bias"][r] = jnp.where(column[:, 0:1] == ids, 0.0, -1e30)
+
+    def attend(r, h):
+        at = pl.ds(h * 256, 256)
+        q_a = buf["mix"][r, at, 0:128]
+        q_b = buf["mix"][r, at, 384:512]
+        zero = jnp.zeros_like(q_a)
+        parts = []
+        for head in range(3):
+            if head == 1:
+                query = jnp.where(low_half, zero, q_a)
+            else:
                 query = jnp.where(low_half, q_b if head == 2 else q_a, zero)
-                if head == 1:
-                    query = jnp.where(low_half, zero, q_a)
-                scores = dot(query, k_b if head == 2 else k_a, 1, 1) + buf["bias"][at, :]
-                top = jnp.max(scores, axis=-1, keepdims=True)
-                expo = jnp.exp(scores - top)
-                probs = expo * (1.0 / jnp.sum(expo, axis=-1, keepdims=True))
-                buf["prob"][r, head, at, :] = probs
-                value = v_a if head < 2 else (v_b if h == 0 else v_b_up)
-                parts.append(dot(probs.astype(BF), value, 1, 0))
-            buf["ctx"][r, at, 0:128] = jnp.where(low_half, parts[0], parts[1]).astype(BF)
-            buf["ctx"][r, at, 128:256] = parts[2].astype(BF)
+            key = buf["mixr"][r] if head == 2 else buf["mix"][r, :, 128:256]
+            value = buf["mix"][r, :, 512:640] if head == 2 else buf["mix"][r, :, 256:384]
+            scores = dot(query, key, 1, 1) + buf["bias"][r, at, :]
+            top = jnp.max(scores, axis=-1, keepdims=True)
+            expo = jnp.exp(scores - top)
+            probs = expo * (1.0 / jnp.sum(expo, axis=-1, keepdims=True))
+            buf["prob"][r, head, at, :] = probs
+            parts.append(dot(probs.astype(BF), value, 1, 0))
+        both = jnp.where(low_half, parts[0], parts[1]).astype(BF)
+        buf["ctx"][r, at, 0:128] = both
+        buf["ctx"][r, at, 128:256] = parts[2].astype(BF)
         for part in range(2):
-            here = [
-                buf["ctx"][r, h * 256 + part * 128 : h * 256 + part * 128 + 128, :]
-                for h in range(2)
-            ]
-            buf["cs"][r, part, 0:128] = here[0][:, 0:128]
-            buf["cs"][r, part, 128:256] = here[1][:, 0:128]
-            buf["cs"][r, part, 256:384] = jnp.where(
-                lane[0:128] < 64, here[0][:, 128:256], here[1][:, 128:256]
-            )
-        ctx_copies.append(
-            [
-                send(buf["cs"].at[r, core], buf["cr"].at[r, me], over),
-                send(buf["cs"].at[r, 1 - core], buf["cr"].at[r, me], over_mate),
-                send(buf["cs"].at[r, 1 - core], buf["cr"].at[r, me], mate),
-            ]
-        )
-        buf["cr"][r, me] = buf["cs"][r, core]
+            first = part * 128
+            buf["cs"][r, h, part, 0:128] = both[first : first + 128]
+            buf["cs"][r, h, part, 128:192] = jnp.where(
+                lane[0:64] < 64,
+                parts[2][first : first + 64],
+                pltpu.roll(parts[2][first + 64 : first + 128], 64, 1),
+            ).astype(BF)
+
+    def send_context(r, h):
+        there = buf["cr"].at[r, h, me]
+        ctx_copies[r, h] = [
+            send(buf["cs"].at[r, h, core], there, over),
+            send(buf["cs"].at[r, h, 1 - core], there, over_mate),
+            send(buf["cs"].at[r, h, 1 - core], there, mate),
+        ]
+        buf["cr"][r, h, me] = buf["cs"][r, h, core]
+
+    weight_copies = {}
+
+    def send_weight():
+        weight_copies["over"] = send(wo_h, buf["wo"].at[me, 0:192], over)
+        weight_copies["mate"] = send(wo_h, buf["wo"].at[me, 0:192], mate)
+
+    def forward_weight():
+        weight_copies["over"].wait_recv()
+        theirs = buf["wo"].at[(1 - chip) * 2 + core, 0:192]
+        weight_copies["far"] = send(theirs, theirs, mate)
+
+    def complete_weight():
+        got_wo.wait()
+        weight_copies["mate"].wait_recv()
+        weight_copies["far"].wait_recv()
+        for group in range(4):
+            buf["wo"][group, 192:256] = buf["wo"][group, 128:192]
 
     flow_copies = {}
 
-    def first_norm(r):
-        for copy in ctx_copies[r]:
+    def first_norm(r, h):
+        for copy in ctx_copies[r, h]:
             copy.wait_recv()
         total = None
         for group in range(4):
-            packed = buf["cr"][r, group, 256:384]
+            packed = buf["cr"][r, h, group, 128:192]
             zero = jnp.zeros_like(packed)
-            keep = lane[0:128] < 64
+            keep = lane[0:64] < 64
             left = jnp.concatenate(
                 [
-                    buf["cr"][r, group, 0:256],
+                    buf["cr"][r, h, group, 0:128],
                     jnp.concatenate(
                         [jnp.where(keep, packed, zero), jnp.where(keep, zero, packed)], axis=0
                     ),
@@ -272,25 +338,26 @@
             )
             term = dot(left, buf["wo"][group], 1, 0).astype(BF).astype(F32)
             total = term if total is None else total + term
-        first_in = buf["tok"][r, :, core].reshape(256, 768).astype(F32) + total + vec[1:2, :]
+        at = pl.ds(h * 128, 128)
+        first_in = buf["tok"][r, h, core].astype(F32) + total + vec[1:2, :]
         center = first_in - mean_of(first_in)
         scale = lax.rsqrt(mean_of(center * center) + EPS)
         unit = center * scale
-        buf["n1"][r] = unit
-        buf["r1"][r] = scale
+        buf["n1"][r, at, :] = unit
+        buf["r1"][r, at, :] = scale
         first_out = unit * vec[2:3, :] + vec[3:4, :]
-        buf["fo"][r] = first_out
-        first_low = first_out.astype(BF)
-        for h in range(2):
-            buf["flow"][r, h, core] = first_low[h * 128 : h * 128 + 128]
-            own = buf["flow"].at[r, h, core]
-            flow_copies[r, h] = send(own, own, mate)
+        buf["fo"][r, at, :] = first_out
+        buf["flow"][r, h, core] = first_out.astype(BF)
+        own = buf["flow"].at[r, h, core]
+        flow_copies[r, h] = send(own, own, mate)
 
     pair_copies = {}
     cross_copies = {}
 
     def ffn_forward(r, h):
         flow_copies[r, h].wait_recv()
+        loaded(got_wu)
+        loaded(got_wd)
         rows_in = buf["flow"][r, h].reshape(256, 768)
         for part in range(3):
             at = pl.ds(part * 256, 256)
@@ -320,6 +387,7 @@
     dsl_copies = {}
 
     def second_norm(r, h):
+        loaded(got_cot)
         total = crossed(2, r, h)
         at = pl.ds(h * 128, 128)
         second_in = buf["fo"][r, at, :] + total + vec[5:6, :]
@@ -342,9 +410,12 @@
         buf["vs"][0:1, :] += row_sum(grad * unit)
         buf["vs"][1:2, :] += row_sum(grad)
         buf["vs"][2:3, :] += row_sum(d_second)
+        finished.append("layer")
+        if finished.count("layer") == 2 * rows:
+            emit(0)
 
     def ffn_backward(r, h):
-        dsl_copies[r, h].wait_recv()
+        arrive(dsl_copies[r, h])
         rows_in = buf["dsl"][r, h].reshape(256, 768)
         for part in range(3):
             at = pl.ds(part * 256, 256)
@@ -376,15 +447,14 @@
 
     def attention_back(r):
         for h in range(2):
-            dal_copies[r, h].wait_recv()
+            arrive(dal_copies[r, h])
         buf["dctx"][...] = dot(
             buf["dal"][r].reshape(512, 768), buf["wo"][me], 1, 1
         ).astype(BF)
         q_a = buf["mix"][r, :, 0:128]
         k_a = buf["mix"][r, :, 128:256]
         v_a = buf["mix"][r, :, 256:384]
-        qk_b = buf["mix"][r, :, 384:512]
-        qk_roll = pltpu.roll(qk_b.astype(F32), 64, 1).astype(BF)
+        qk_roll = buf["mixr"][r]
         v_b = buf["mix"][r, :, 512:640]
         d_q, d_k, d_v = [], [], []
         for head in range(3):
@@ -447,53 +517,79 @@
         total = pair + buf["x4r"][h].astype(F32)
         result = buf["dfi"][chip, pl.ds(h * 128, 128), :] + total
         outs[1][h * 128 : h * 128 + 128, :] = result.astype(BF)
-
-    first_copies = {}
-    second_copies = {}
+        finished.append("token")
+        if finished.count("token") == 2:
+            emit(1)
+
+    steps = {}
     starts = {}
     column = 0
     for name, width in PIECES:
         starts[name] = column
         column += width
-
-    def reduce_start(name, grad):
+    finished = []
+
+    def piece(name):
+        return [buf[kind + name] for kind in ("g_", "a_", "s_", "b_", "v_", "c_")]
+
+    def reduce_start(name):
+        grad = gradient(name)
         width = dict(PIECES)[name]
         if not fused:
             outs[2][:, starts[name] : starts[name] + width] = grad
+            finished.append(name)
+            if len(set(finished) & set(starts)) == len(PIECES):
+                emit(2)
             return
-        stage = buf["g_" + name]
+        stage, came = piece(name)[:2]
         stage[...] = grad.astype(BF).reshape(stage.shape)
-        first_copies[name] = send(
-            stage.at[:, 1 - why], buf["a_" + name], (zed * 2 + (1 - why), me)
-        )
-
-    def reduce_middle(name):
+        if name in DEPTH_FIRST:
+            steps[name] = send(stage.at[:, 1 - near], came, next_near)
+        else:
+            steps[name] = send(stage.at[:, :, 1 - why], came, side)
+
+    def reduce_first(name):
         if not fused:
             return
-        first_copies[name].wait_recv()
-        stage, came = buf["g_" + name], buf["a_" + name]
-        copies = []
-        for step in range(1, half):
-            target = lax.rem(zed + step, half)
-            both = stage[target, why].astype(F32) + came[target].astype(F32)
-            buf["s_" + name][step - 1] = both.astype(BF)
-            copies.append(
-                send(
-                    buf["s_" + name].at[step - 1],
-                    buf["b_" + name].at[step - 1],
-                    row_partner(step),
-                )
-            )
-        second_copies[name] = copies
-        buf["t_" + name][...] = stage[zed, why].astype(F32) + came[zed].astype(F32)
+        steps[name].wait_recv()
+        stage, came, out, into = piece(name)[:4]
+        for at in range(2):
+            if name in DEPTH_FIRST:
+                total = stage[1 - far, near, at].astype(F32) + came[1 - far, at].astype(F32)
+            else:
+                total = stage[at, 1 - near, why].astype(F32) + came[at, 1 - near].astype(F32)
+            out[at] = total.astype(BF)
+        steps[name] = send(out, into, next_far if name in DEPTH_FIRST else next_near)
+
+    def reduce_second(name):
+        if not fused:
+            return
+        steps[name].wait_recv()
+        stage, came, _, into, out, last = piece(name)
+        if name in DEPTH_FIRST:
+            total = stage[far, near, 1 - why].astype(F32) + came[far, 1 - why].astype(F32)
+            total = total + into[1 - why].astype(F32)
+        else:
+            total = stage[1 - far, near, why].astype(F32) + came[1 - far, near].astype(F32)
+            total = total + into[1 - far].astype(F32)
+        out[...] = total.astype(BF)
+        steps[name] = send(out, last, side if name in DEPTH_FIRST else next_far)
+
+    def emit(*which):
+        for at in which:
+            stored.append(fetch(outs[at], results[at]))
 
     def reduce_finish(name):
         if not fused:
             return
-        total = buf["t_" + name][...]
-        for step, copy in enumerate(second_copies[name]):
-            copy.wait_recv()
-            total = total + buf["b_" + name][step].astype(F32)
+        steps[name].wait_recv()
+        stage, came, _, into, _, last = piece(name)
+        total = stage[far, near, why].astype(F32)
+        if name in DEPTH_FIRST:
+            total = total + came[far, why].astype(F32) + into[why].astype(F32)
+        else:
+            total = total + came[far, near].astype(F32) + into[far].astype(F32)
+        total = total + last[...].astype(F32)
         if name[0] == "d":
             outs[10][:, starts[name] : starts[name] + 256] = total
         elif name[0] == "u":
@@ -506,16 +602,25 @@
                 outs[2][kind * 192 : kind * 192 + 128, :] = total[
                     :, kind * 128 : kind * 128 + 128
                 ].T
+        elif name == "r":
+            flipped = total.T
+            outs[2][128:192, :] = flipped[0:64]
+            outs[2][320:384, :] = flipped[64:128]
         else:
-            for at in range(4):
-                flipped = total[:, (at // 2) * 128 : (at // 2) * 128 + 128].T
-                piece = flipped[(at % 2) * 64 : (at % 2) * 64 + 64]
-                if at < 3:
-                    outs[2][at * 192 + 128 : at * 192 + 192, :] = piece
-                else:
-                    outs[4][128:192, :] = piece
+            flipped = total.T
+            outs[2][512:576, :] = flipped[0:64]
+            outs[4][128:192, :] = flipped[64:128]
+        before = set(finished)
+        finished.append(name)
+        for group, at in (("d0 d1 d2", 10), ("u0 u1 u2", 8), ("q r s", 2), ("o s", 4)):
+            wanted = set(group.split())
+            if wanted <= set(finished) and not wanted <= before:
+                emit(at)
 
     def down_grad(part):
+        for r in range(rows):
+            for h in range(2):
+                arrive(dsl_copies[r, h])
         at = pl.ds(part * 256, 256)
         return dot(
             buf["dsl"][...].reshape(rows * 512, 768),
@@ -533,7 +638,13 @@
             0,
         )
 
+    def all_back():
+        for r in range(rows):
+            for h in range(2):
+                arrive(dal_copies[r, h])
+
     def out_grad_first():
+        all_back()
         return dot(
             buf["dal"][...].reshape(rows * 512, 768),
             buf["ctx"][:, :, 0:128].reshape(rows * 512, 128),
@@ -542,17 +653,14 @@
         )
 
     def out_grad_second():
-        sides = []
-        for h in range(2):
-            sides.append(
-                dot(
-                    buf["dal"][:, h].reshape(rows * 256, 768),
-                    buf["ctx"][:, h * 256 : h * 256 + 256, 128:256].reshape(rows * 256, 128),
-                    0,
-                    0,
-                )
-            )
-        return pltpu.roll(sides[0], 64, 1) + sides[1]
+        all_back()
+        turned = dot(
+            buf["dal"][...].reshape(rows * 512, 768),
+            buf["ctx"][:, :, 128:256].reshape(rows * 512, 128),
+            0,
+            0,
+        )
+        return pltpu.roll(turned, 64, 1)
 
     def qkv_grad(low, high):
         return dot(
@@ -562,111 +670,55 @@
             0,
         )
 
-    attention(0)
-    wo_over.wait_recv()
-    theirs = buf["wo"].at[(1 - chip) * 2 + core, 0:192]
-    wo_far = send(theirs, theirs, mate)
-    attention(1)
-    wo_mate.wait_recv()
-    wo_far.wait_recv()
-    for group in range(4):
-        buf["wo"][group, 192:256] = buf["wo"][group, 128:192]
-    first_norm(0)
-    got_wu.wait()
-    got_wd.wait()
-    got_cot.wait()
-    ffn_forward(0, 0)
-    ffn_forward(0, 1)
-    exchange(2, 0, 0)
-    first_norm(1)
-    exchange(2, 0, 1)
-    ffn_forward(1, 0)
-    ffn_forward(1, 1)
-    exchange(2, 1, 0)
-    second_norm(0, 0)
-    exchange(2, 1, 1)
-    ffn_backward(0, 0)
-    second_norm(0, 1)
-    exchange(3, 0, 0)
-    ffn_backward(0, 1)
-    second_norm(1, 0)
-    exchange(3, 0, 1)
-    ffn_backward(1, 0)
-    second_norm(1, 1)
-    exchange(3, 1, 0)
-    ffn_backward(1, 1)
-    reduce_start("d0", down_grad(0))
-    exchange(3, 1, 1)
-    reduce_start("u0", up_grad(0))
-    reduce_start("d1", down_grad(1))
-    first_norm_back(0, 0)
-    reduce_start("u1", up_grad(1))
-    reduce_start("d2", down_grad(2))
-    reduce_middle("d0")
-    first_norm_back(0, 1)
-    reduce_start("u2", up_grad(2))
-    reduce_middle("u0")
-    attention_back(0)
-    reduce_middle("d1")
-    token_terms(0, 0)
-    token_terms(0, 1)
-    token_cross(0, 0)
-    first_norm_back(1, 0)
-    token_cross(0, 1)
-    reduce_middle("u1")
-    first_norm_back(1, 1)
-    attention_back(1)
-    token_terms(1, 0)
-    token_terms(1, 1)
-    reduce_start("o", out_grad_first())
-    token_cross(1, 0)
-    reduce_start("q", qkv_grad(0, 384))
-    token_cross(1, 1)
-    tail = qkv_grad(384, 640)
-    merged = jnp.concatenate(
-        [
-            tail[:, 0:128],
-            jnp.where(
-                lax.broadcasted_iota(jnp.int32, (768, 128), 1) < 64,
-                tail[:, 128:256],
-                out_grad_second(),
-            ),
-        ],
-        axis=1,
-    )
-    reduce_start("r", merged)
-
-    vec_mate = send(buf["vs"], buf["vm"], mate)
-    reduce_middle("d2")
-    reduce_middle("u2")
-    vec_mate.wait_recv()
-    shared = lax.broadcasted_iota(jnp.int32, (8, 768), 0) < 6
-    small = buf["vs"][...] + jnp.where(shared, buf["vm"][...], 0.0)
-    if fused:
+    def gradient(name):
+        if name[0] == "d":
+            return down_grad(int(name[1]))
+        if name[0] == "u":
+            return up_grad(int(name[1]))
+        if name == "o":
+            return out_grad_first()
+        if name == "q":
+            return qkv_grad(0, 384)
+        if name == "r":
+            return qkv_grad(384, 512)
+        first = lax.broadcasted_iota(jnp.int32, (768, 128), 1) < 64
+        return jnp.where(first, qkv_grad(512, 640), out_grad_second())
+
+    small_copies = {}
+
+    def small_mate():
+        small_copies["mate"] = send(buf["vs"], buf["vm"], mate)
+
+    def small_side():
+        small_copies["mate"].wait_recv()
+        shared = lax.broadcasted_iota(jnp.int32, (8, 768), 0) < 6
+        small = buf["vs"][...] + jnp.where(shared, buf["vm"][...], 0.0)
+        if not fused:
+            outs[3][...] = small
+            emit(3)
+            return
         buf["vt"][...] = small
-        vec_row = send(buf["vt"], buf["vy"], (zed * 2 + (1 - why), me))
-    else:
-        outs[3][...] = small
-    for name in ("d0", "u0", "d1", "u1"):
-        reduce_finish(name)
-    reduce_middle("o")
-    reduce_middle("q")
-    reduce_middle("r")
-    if fused:
-        vec_row.wait_recv()
-        vec_row.wait_send()
-        pending[:] = [copy for copy in pending if copy is not vec_row]
-        small = small + buf["vy"][...]
-        buf["vt"][...] = small
-        vec_far = [send(buf["vt"], buf["vz"].at[s - 1], row_partner(s)) for s in range(1, half)]
-    token_finish(0)
-    token_finish(1)
-    for name in ("d2", "u2", "o"):
-        reduce_finish(name)
-    if fused:
-        for step, copy in enumerate(vec_far):
-            copy.wait_recv()
-            small = small + buf["vz"][step]
+        small_copies["side"] = send(buf["vt"], buf["vy"], side)
+
+    def small_near():
+        if not fused:
+            return
+        small_copies["side"].wait_recv()
+        buf["vu"][...] = buf["vt"][...] + buf["vy"][...]
+        small_copies["near"] = send(buf["vu"], buf["vz"], next_near)
+
+    def small_far():
+        if not fused:
+            return
+        small_copies["near"].wait_recv()
+        buf["vw"][...] = buf["vu"][...] + buf["vz"][...]
+        small_copies["far"] = send(buf["vw"], buf["vx"], next_far)
+
+    def small_finish():
+        if not fused:
+            return
+        small_copies["far"].wait_recv()
+        small = buf["vw"][...] + buf["vx"][...]
         share = 768 // n_dp
         turned = pltpu.roll(small, 768 - dp * share, 1)
         for row, at in ((5, 5), (3, 6), (4, 7), (2, 11), (0, 12), (1, 13)):
@@ -690,10 +742,111 @@
         heads = jnp.dot(spread, pick, precision=lax.Precision.HIGHEST)
         for head in range(3):
             outs[3][head] = heads[head * 2 : head * 2 + 2, 0:wide]
+        emit(3, 5, 6, 7, 9, 11, 12, 13)
+
+    project(1)
+    attend(1, 1)
+    project(0)
+    pl.semaphore_wait(barrier, len(partners))
+    send_weight()
+    attend(0, 1)
+    send_context(1, 1)
+    attend(1, 0)
+    send_context(1, 0)
+    attend(0, 0)
+    send_context(0, 0)
+    send_context(0, 1)
+    forward_weight()
+    complete_weight()
+    first_norm(1, 1)
+    ffn_forward(1, 1)
+    first_norm(1, 0)
+    first_norm(0, 0)
+    exchange(2, 1, 1)
+    ffn_forward(1, 0)
+    first_norm(0, 1)
+    ffn_forward(0, 0)
+    exchange(2, 1, 0)
+    ffn_forward(0, 1)
+    exchange(2, 0, 0)
+    exchange(2, 0, 1)
+    second_norm(1, 1)
+    ffn_backward(1, 1)
+    exchange(3, 1, 1)
+    second_norm(1, 0)
+    ffn_backward(1, 0)
+    second_norm(0, 0)
+    exchange(3, 1, 0)
+    ffn_backward(0, 0)
+    second_norm(0, 1)
+    exchange(3, 0, 0)
+    reduce_start("d1")
+    reduce_start("d0")
+    reduce_start("d2")
+    ffn_backward(0, 1)
+    reduce_start("u1")
+    reduce_start("u0")
+    exchange(3, 0, 1)
+    reduce_start("u2")
+    first_norm_back(1, 1)
+    first_norm_back(1, 0)
+    reduce_first("d1")
+    reduce_first("d0")
+    attention_back(1)
+    first_norm_back(0, 0)
+    reduce_first("d2")
+    token_terms(1, 1)
+    reduce_first("u2")
+    token_terms(1, 0)
+    token_cross(1, 1)
+    token_cross(1, 0)
+    first_norm_back(0, 1)
+    reduce_first("u1")
+    reduce_second("d0")
+    reduce_start("o")
+    attention_back(0)
+    reduce_start("q")
+    reduce_second("d2")
+    reduce_first("u0")
+    token_terms(0, 0)
+    small_mate()
+    reduce_start("s")
+    reduce_second("u1")
+    reduce_second("d1")
+    token_terms(0, 1)
+    token_cross(0, 0)
+    reduce_second("u2")
+    small_side()
+    reduce_start("r")
+    reduce_first("o")
+    token_cross(0, 1)
+    reduce_finish("d0")
+    reduce_finish("d2")
+    reduce_second("u0")
+    reduce_first("q")
+    token_finish(0)
+    reduce_second("o")
+    reduce_finish("u1")
+    reduce_first("s")
+    reduce_finish("d1")
+    reduce_finish("u0")
+    reduce_finish("u2")
+    token_finish(1)
+    small_near()
+    reduce_second("q")
+    reduce_first("r")
+    reduce_second("s")
+    reduce_finish("o")
+    small_far()
+    reduce_second("r")
     reduce_finish("q")
+    reduce_finish("s")
+    small_finish()
     reduce_finish("r")
     for copy in pending + cross4:
         copy.wait_send()
+    for copy in stored:
+        copy.wait()
 
 
 def body(
@@ -716,26 +869,8 @@
     rows = tokens.shape[0] // SEQ
     n_dp = lax.axis_size("dp")
     share = 768 // n_dp
-    fused = share % 16 == 0 and n_dp % 2 == 0
+    fused = n_dp == 8
     split = (rows, 2, 2, 128, 768)
-    pad = jnp.zeros((64,), BF)
-    bias_q = qkv_bias[0].reshape(192)
-    bias_v = qkv_bias[1].reshape(192)
-    vectors = jnp.stack(
-        [
-            jnp.concatenate(
-                [bias_q[:128], pad, pad, bias_v[:128], bias_q[128:], pad, bias_v[128:], pad, pad, pad]
-            ),
-            output_bias,
-            first_gain,
-            first_shift,
-            up_bias.reshape(768),
-            down_bias,
-            second_gain,
-            second_shift,
-        ]
-    ).astype(F32)
-    plan = scratch_plan(rows, n_dp // 2, fused)
     shape = jax.ShapeDtypeStruct
     outs = [shape((256, 768), BF), shape((256, 768), BF)]
     if fused:
@@ -757,7 +892,7 @@
         ]
     else:
         outs += [shape((768, 2304), F32), shape((8, 768), F32)]
-    whole = pl.BlockSpec(memory_space=pltpu.VMEM)
+    plan = scratch_plan(rows, share, fused, outs)
     anywhere = pl.BlockSpec(memory_space=pl.ANY)
 
     def kernel(*refs):
@@ -766,8 +901,8 @@
     got = pl.pallas_call(
         kernel,
         out_shape=outs,
-        in_specs=[anywhere] * 6 + [whole] * 2,
-        out_specs=[whole] * len(outs),
+        in_specs=[anywhere] * INPUTS,
+        out_specs=[anywhere] * len(outs),
         scratch_shapes=[pltpu.VMEM(dims, kind) for dims, kind in plan.values()]
         + [
             pltpu.SemaphoreType.DMA((LOCAL_COPIES,)),
@@ -785,9 +920,23 @@
         up_weight,
         down_weight,
         segment_ids,
-        vectors,
+        qkv_bias.transpose(1, 0, 2),
+        up_bias,
+        *(
+            vector.reshape(6, 128)
+            for vector in (
+                output_bias,
+                first_gain,
+                first_shift,
+                down_bias,
+                second_gain,
+                second_shift,
+            )
+        ),
     )
-    if not fused:
+    if fused:
+        got = hand_over(got)
+    else:
         got = finish_plain(n_dp, *got)
     return (
         got[0],
@@ -805,6 +954,37 @@
         got[12].reshape(share),
         got[13].reshape(share),
     )
+
+
+def hand_over(arrays):
+    count = len(arrays)
+
+    def kernel(*refs):
+        source, result, held = (refs[at * count : at * count + count] for at in range(3))
+        sem = refs[3 * count]
+        inward = [
+            pltpu.make_async_copy(source[at], held[at], sem.at[at]) for at in range(count)
+        ]
+        outward = [
+            pltpu.make_async_copy(held[at], result[at], sem.at[count + at]) for at in range(count)
+        ]
+        for copy in inward:
+            copy.start()
+        for before, after in zip(inward, outward):
+            before.wait()
+            after.start()
+        for copy in outward:
+            copy.wait()
+
+    anywhere = pl.BlockSpec(memory_space=pl.ANY)
+    return pl.pallas_call(
+        kernel,
+        out_shape=[jax.ShapeDtypeStruct(a.shape, a.dtype) for a in arrays],
+        in_specs=[anywhere] * count,
+        out_specs=[anywhere] * count,
+        scratch_shapes=[pltpu.VMEM(a.shape, a.dtype) for a in arrays]
+        + [pltpu.SemaphoreType.DMA((2 * count,))],
+    )(*arrays)
 
 
 def finish_plain(n_dp, layer, tokens_grad, grads, small):

time: 122 us -> 99.3 us (0.81)
  local copies, waits for them, and re-layouts: 17.4 us -> 0 us
  Pallas kernels: 103 us -> 98.3 us
    unnamed x38 -> x0, local copies, waits for them, and re-layouts: 10.7 us -> none
    another operation x9 -> x0, local copies, waits for them, and re-layouts: 4.94 us -> none  [body(): jnp.stack([jnp.concatenate([bias_q[:128], pad, pad, bias_v[:128], bias_q[...]
    pallas_call x1 -> x2, Pallas kernels: 103 us -> 98.3 us  [the longest x1 95.8 us: body(): pl.pallas_call(kernel, out_shape=outs, in_specs=[anywhere] * INPUTS, out_...]
    slice x4 -> x0, local copies, waits for them, and re-layouts: 1.68 us -> none  [the longest x2 0.86 us: body(): bias_v[:128]]
where the time goes in v2:
time: 99.3 us; the launch traced here: 99.1 us
  Pallas kernels  98.3 us (99%)
    pallas_call x1, Pallas kernels, body(): pl.pallas_call(kernel, out_shape=outs, in_specs=[anywhere] * INPUTS, out_...  95.8 us
    pallas_call x1, Pallas kernels, hand_over(): pl.pallas_call(kernel, out_shape=[jax.ShapeDtypeStruct(a.shape, a.dtype)...  2.48 us

profile of v2, /device:TPU:0, one launch (start us, length us, event | category | flops | bytes accessed | tf_op | source)
XLA Modules:
  0.0 99.1 jit_solution(10309248313225592285)
XLA Ops:
  0.7 95.8 %shard_map.254 = (bf16[256,768]{1,0:T(8,128)(2,1)}, bf16[256,768]{1,0:T(8,128)(2,1)}, f32[576,96]{1,0:T(8,128)}, f32[3,2,8]{2,1,0:T(2,128)}, f32[192,96]{1,0:T(8...) custom-call(bf16[2,2,2,128,768]{4,3,2,1,0:T(8,128)(2,1)} %bitcast.26, ...), custom_call_target="tpu_custom_call" | custom-call | tf_op jit(solution)/shard_map/pallas_call | solution.py:901
  96.5 2.5 %shard_map.255 = (bf16[256,768]{1,0:T(8,128)(2,1)}, bf16[256,768]{1,0:T(8,128)(2,1)}, f32[576,96]{1,0:T(8,128)}, f32[3,2,8]{2,1,0:T(2,128)}, f32[192,96]{1,0:T(8...) custom-call(bf16[256,768]{1,0:T(8,128)(2,1)} %get-tuple-element.42.r, ...), custom_call_target="tpu_custom_call" | custom-call | tf_op jit(solution)/shard_map/pallas_call | solution.py:980

commit v3 on v2

v3 whole, which is shorter than its diff:
```python
from types import SimpleNamespace

import jax
import jax.numpy as jnp
from jax import lax
from jax.experimental import pallas as pl
from jax.experimental.pallas import tpu as pltpu
from jax.sharding import PartitionSpec as P

HEAD = 64
SEQ = 512
EPS = 1e-12
SCALE = HEAD ** (-0.5)
BF = jnp.bfloat16
F32 = jnp.float32
MESH_ID = pl.DeviceIdType.MESH
NAMES = ("dp", "tensor")
D0, D1, D2, U0, U1, U2, OUT, QK, V, QK2, V2 = range(11)
WIDTHS = (256, 256, 256, 256, 256, 256, 128, 256, 128, 128, 128)
DEPTH_FIRST = (D0, U2)


def dot(left, right, left_dim, right_dim):
    return lax.dot_general(
        left, right, (((left_dim,), (right_dim,)), ((), ())), preferred_element_type=F32
    )


def mean_of(values):
    return jnp.mean(values, axis=-1, keepdims=True)


def row_sum(values):
    return jnp.sum(values, axis=0, keepdims=True)


def scratch_plan(rows, share, fused, results):
    plan = dict(
        seg=((rows, SEQ), jnp.int32),
        bqv=((3, 2, HEAD), BF),
        bup=((12, HEAD), BF),
        vec=((8, 768), F32),
        tok=((rows, 2, 2, 128, 768), BF),
        cot=((rows, 2, 128, 768), BF),
        wq=((5, 128, 768), BF),
        wo=((4, 256, 768), BF),
        wu=((768, 768), BF),
        wd=((768, 768), BF),
        mix=((rows, 512, 640), BF),
        bias=((rows, 512, 512), F32),
        mixr=((rows, 512, 128), BF),
        prob=((rows, 3, 512, 512), F32),
        ctx=((rows, 512, 256), BF),
        cs=((rows, 2, 2, 192, 128), BF),
        cr=((rows, 2, 4, 192, 128), BF),
        n1=((rows, 256, 768), F32),
        r1=((rows, 256, 1), F32),
        fo=((rows, 256, 768), F32),
        flow=((rows, 2, 2, 128, 768), BF),
        act=((rows, 2, 256, 768), BF),
        gp=((rows, 2, 256, 768), F32),
        ds=((rows, 256, 768), F32),
        dsl=((rows, 2, 2, 128, 768), BF),
        dhl=((rows, 2, 256, 768), BF),
        dfi=((rows, 256, 768), F32),
        dal=((rows, 2, 2, 128, 768), BF),
        dctx=((512, 256), BF),
        dsc=((3, 512, 512), BF),
        dmx=((rows, 512, 640), BF),
        x4=((2, 128, 768), BF),
        x4r=((2, 128, 768), BF),
        vs=((8, 768), F32),
        vm=((8, 768), F32),
    )
    plan.update(
        pair=[((rows, 2, 2, 128, 768), BF)] * 3,
        paired=[((rows, 2, 128, 768), BF)] * 3,
        cross=[((rows, 2, 128, 768), BF)] * 2,
        crossed=[((rows, 2, 128, 768), BF)] * 2,
        given=[((6, 128), BF)] * 6,
        outs=[(result.shape, result.dtype) for result in results],
    )
    if fused:
        plan.update(
            small=[((8, 768), F32)] * 6,
            pieces=[
                [
                    ((2, 2, 2, share, width), BF),
                    ((2, 2, share, width), BF),
                    ((2, share, width), BF),
                    ((2, share, width), BF),
                    ((share, width), BF),
                    ((share, width), BF),
                ]
                for width in WIDTHS
            ],
        )
    return plan


def is_buffer(node):
    return isinstance(node, tuple)


INPUTS = 15
OVER, CORNER, PAIR, ROWS, CROSS = range(5)
FIRST_ROW = 0
LOCAL_COPIES = 21
REMOTE_COPIES = 60


def layer_kernel(rows, n_dp, fused, tree, *refs):
    tok_h, cot_h, wq_h, wo_h, wu_h, wd_h, seg_h = refs[:7]
    small_h = refs[7:INPUTS]
    n_out = 14 if fused else 4
    results = refs[INPUTS : INPUTS + n_out]
    held = tree.num_leaves
    buf = SimpleNamespace(
        **jax.tree.unflatten(tree, refs[INPUTS + n_out : INPUTS + n_out + held])
    )
    outs, seg, vec = buf.outs, buf.seg, buf.vec
    local_sem, send_sem, recv_sem = refs[INPUTS + n_out + held :]

    dp = lax.axis_index("dp")
    me = lax.axis_index("tensor")
    chip = me // 2
    core = lax.rem(me, 2)
    mate = (dp, chip * 2 + (1 - core))
    over = (dp, (1 - chip) * 2 + core)
    over_mate = (dp, (1 - chip) * 2 + (1 - core))
    why = lax.rem(dp, 2)
    near = lax.rem(dp // 2, 2)
    far = dp // 4
    side = (dp + 1 - 2 * why, me)
    next_near = (dp + 2 - 4 * near, me)
    next_far = (dp + 4 - 8 * far, me)

    fetched = []
    stored, token_rows, layer_rows = [], [], []

    def fetch(src, dst, at=None):
        if at is None:
            at = len(fetched)
            fetched.append(at)
        copy = pltpu.make_async_copy(src, dst, local_sem.at[at])
        copy.start()
        return copy

    keys = {}
    latest = {}

    def remote(src, dst, device, key):
        at = keys.setdefault(key, len(keys))
        copy = pltpu.make_async_remote_copy(
            src_ref=src,
            dst_ref=dst,
            send_sem=send_sem.at[at],
            recv_sem=recv_sem.at[at],
            device_id=device,
            device_id_type=MESH_ID,
        )
        if key in latest:
            latest[key].wait_send()
        latest[key] = copy
        return copy

    arrived = []

    def once(copy):
        new = not any(copy is other for other in arrived)
        if new:
            arrived.append(copy)
        return new

    def arrive(copy):
        if once(copy):
            copy.wait_recv()

    def loaded(copy):
        if once(copy):
            copy.wait()

    def send(src, dst, device, key):
        copy = remote(src, dst, device, key)
        copy.start()
        return copy

    partners = [mate, over, over_mate]
    if fused:
        partners += [side, next_near, next_far]
    barrier = pltpu.get_barrier_semaphore()
    for device in partners:
        pl.semaphore_signal(barrier, inc=1, device_id=device, device_id_type=MESH_ID)
    got_tok = [None] * rows

    def fetch_row(r):
        got_tok[r] = [fetch(tok_h.at[r, :, h], buf.tok.at[r, h]) for h in range(2)]

    lane = lax.broadcasted_iota(jnp.int32, (256, 128), 1)
    low_half = lane < 64
    lane_row = lax.broadcasted_iota(jnp.int32, (512, 128), 1) < 64
    later = SimpleNamespace()

    def fetch_all():
        fetch_row(FIRST_ROW)
        later.wq = [
            fetch(wq_h.at[:, 0:128], buf.wq.at[0:3]),
            fetch(wq_h.at[0, 128:192], buf.wq.at[3, 0:64]),
            fetch(wq_h.at[1, 128:192], buf.wq.at[3, 64:128]),
            fetch(wq_h.at[2, 128:192], buf.wq.at[4, 0:64]),
        ]
        later.small = [fetch(seg_h, buf.seg), fetch(small_h[0], buf.bqv)]
        later.small.append(fetch(small_h[1], buf.bup))
        later.small += [fetch(small_h[2 + at], buf.given[at]) for at in range(6)]
        for r in range(rows):
            if r != FIRST_ROW:
                fetch_row(r)
        later.wo = fetch(wo_h, buf.wo.at[me, 0:192])
        later.wu = fetch(wu_h, buf.wu)
        later.wd = fetch(wd_h, buf.wd)
        later.cot = fetch(cot_h.at[:, core], buf.cot)

    def prepare():
        fetch_all()
        buf.wq[4, 64:128] = jnp.zeros((64, 768), BF)
        buf.vs[...] = jnp.zeros((8, 768), F32)
        for copy in later.small:
            copy.wait()
        bias = [[buf.bqv[head, kind : kind + 1, :].astype(F32) for kind in range(2)] for head in range(3)]
        none = jnp.zeros((1, HEAD), F32)
        none2 = jnp.zeros((1, 128), F32)
        for at, pair in enumerate(
            (
                (bias[0][0], bias[1][0]),
                (none, none),
                (bias[0][1], bias[1][1]),
                (bias[2][0], none),
                (bias[2][1], none),
            )
        ):
            vec[0:1, at * 128 : at * 128 + 128] = jnp.concatenate(pair, axis=1)
        vec[0:1, 640:768] = none2
        for at in range(6):
            pair = buf.bup[2 * at : 2 * at + 2, :].astype(F32)
            vec[4:5, at * 128 : at * 128 + 128] = jnp.concatenate([pair[0:1], pair[1:2]], axis=1)
        for at, row in enumerate((1, 2, 3, 5, 6, 7)):
            short = buf.given[at][...].astype(F32)
            for part in range(6):
                vec[row : row + 1, part * 128 : part * 128 + 128] = short[part : part + 1]

    ctx_copies = {}

    def project(r):
        for copy in got_tok[r]:
            copy.wait()
        for copy in later.wq:
            loaded(copy)
        mixed = dot(
            buf.tok[r].reshape(512, 768), buf.wq[...].reshape(640, 768), 1, 1
        ) + vec[0:1, 0:640]
        q_low = mixed[:, 0:128].astype(BF).astype(F32) * SCALE
        buf.mix[r, :, 0:128] = q_low.astype(BF)
        buf.mix[r, :, 128:384] = mixed[:, 128:384].astype(BF)
        tail = mixed[:, 384:512].astype(BF).astype(F32)
        tail = jnp.where(lane_row, tail * SCALE, tail)
        buf.mix[r, :, 384:512] = tail.astype(BF)
        buf.mixr[r] = pltpu.roll(tail, 64, 1).astype(BF)
        buf.mix[r, :, 512:640] = mixed[:, 512:640].astype(BF)

        ids = seg[r : r + 1, :].astype(F32)
        ids = jnp.concatenate(
            [ids[:, 0:128], ids[:, 256:384], ids[:, 128:256], ids[:, 384:512]], axis=1
        )
        column = jnp.broadcast_to(ids, (128, 512)).T
        buf.bias[r] = jnp.where(column[:, 0:1] == ids, 0.0, -1e30)

    def attend(r, h):
        at = pl.ds(h * 256, 256)
        q_a = buf.mix[r, at, 0:128]
        q_b = buf.mix[r, at, 384:512]
        zero = jnp.zeros_like(q_a)
        parts = []
        for head in range(3):
            if head == 1:
                query = jnp.where(low_half, zero, q_a)
            else:
                query = jnp.where(low_half, q_b if head == 2 else q_a, zero)
            key = buf.mixr[r] if head == 2 else buf.mix[r, :, 128:256]
            value = buf.mix[r, :, 512:640] if head == 2 else buf.mix[r, :, 256:384]
            scores = dot(query, key, 1, 1) + buf.bias[r, at, :]
            top = jnp.max(scores, axis=-1, keepdims=True)
            expo = jnp.exp(scores - top)
            probs = expo * (1.0 / jnp.sum(expo, axis=-1, keepdims=True))
            buf.prob[r, head, at, :] = probs
            parts.append(dot(probs.astype(BF), value, 1, 0))
        both = jnp.where(low_half, parts[0], parts[1]).astype(BF)
        buf.ctx[r, at, 0:128] = both
        buf.ctx[r, at, 128:256] = parts[2].astype(BF)
        for part in range(2):
            first = part * 128
            buf.cs[r, h, part, 0:128] = both[first : first + 128]
            buf.cs[r, h, part, 128:192] = jnp.where(
                lane[0:64] < 64,
                parts[2][first : first + 64],
                pltpu.roll(parts[2][first + 64 : first + 128], 64, 1),
            ).astype(BF)

    def send_context(r, h):
        there = buf.cr.at[r, h, me]
        ctx_copies[r, h] = [
            send(buf.cs.at[r, h, core], there, over, (OVER, r, h)),
            send(buf.cs.at[r, h, 1 - core], there, over_mate, (CORNER, r, h)),
            send(buf.cs.at[r, h, 1 - core], there, mate, (PAIR, r, h)),
        ]
        buf.cr[r, h, me] = buf.cs[r, h, core]

    weight_copies = SimpleNamespace()

    def send_weight():
        weight_copies.over = send(wo_h, buf.wo.at[me, 0:192], over, 0)
        weight_copies.mate = send(wo_h, buf.wo.at[me, 0:192], mate, 1)

    def forward_weight():
        weight_copies.over.wait_recv()
        theirs = buf.wo.at[(1 - chip) * 2 + core, 0:192]
        weight_copies.far = send(theirs, theirs, mate, 2)

    def complete_weight():
        later.wo.wait()
        weight_copies.mate.wait_recv()
        weight_copies.far.wait_recv()
        for group in range(4):
            buf.wo[group, 192:256] = buf.wo[group, 128:192]

    flow_copies = {}

    def first_norm(r, h):
        for copy in ctx_copies[r, h]:
            copy.wait_recv()
        total = None
        for group in range(4):
            packed = buf.cr[r, h, group, 128:192]
            zero = jnp.zeros_like(packed)
            keep = lane[0:64] < 64
            left = jnp.concatenate(
                [
                    buf.cr[r, h, group, 0:128],
                    jnp.concatenate(
                        [jnp.where(keep, packed, zero), jnp.where(keep, zero, packed)], axis=0
                    ),
                ],
                axis=1,
            )
            term = dot(left, buf.wo[group], 1, 0).astype(BF).astype(F32)
            total = term if total is None else total + term
        at = pl.ds(h * 128, 128)
        first_in = buf.tok[r, h, core].astype(F32) + total + vec[1:2, :]
        center = first_in - mean_of(first_in)
        scale = lax.rsqrt(mean_of(center * center) + EPS)
        unit = center * scale
        buf.n1[r, at, :] = unit
        buf.r1[r, at, :] = scale
        first_out = unit * vec[2:3, :] + vec[3:4, :]
        buf.fo[r, at, :] = first_out
        buf.flow[r, h, core] = first_out.astype(BF)
        own = buf.flow.at[r, h, core]
        flow_copies[r, h] = send(own, own, mate, (ROWS, r, h))

    pair_copies = {}
    cross_copies = {}

    def ffn_forward(r, h):
        flow_copies[r, h].wait_recv()
        loaded(later.wu)
        loaded(later.wd)
        rows_in = buf.flow[r, h].reshape(256, 768)
        for part in range(3):
            at = pl.ds(part * 256, 256)
            hidden = dot(rows_in, buf.wu[:, at], 1, 0) + vec[4:5, at]
            phi = 0.5 * (1.0 + lax.erf(hidden * 0.7071067811865476))
            buf.act[r, h, :, at] = (hidden * phi).astype(BF)
            buf.gp[r, h, :, at] = (
                phi + hidden * jnp.exp(-0.5 * hidden * hidden) * 0.3989422804014327
            )
        terms = dot(buf.act[r, h], buf.wd[...], 1, 0).astype(BF)
        buf.pair[0][r, h] = terms.reshape(2, 128, 768)
        pair_copies[2, r, h] = send(
            buf.pair[0].at[r, h, 1 - core], buf.paired[0].at[r, h], mate, (PAIR, r, h)
        )

    def exchange(stage, r, h):
        pair_copies[stage, r, h].wait_recv()
        own = buf.pair[stage - 2][r, h, core].astype(F32)
        other = buf.paired[stage - 2][r, h].astype(F32)
        buf.cross[stage - 2][r, h] = (own + other).astype(BF)
        cross_copies[stage, r, h] = send(
            buf.cross[stage - 2].at[r, h],
            buf.crossed[stage - 2].at[r, h],
            over,
            (CROSS if stage == 2 else OVER, r, h),
        )

    def crossed(stage, r, h):
        cross_copies[stage, r, h].wait_recv()
        return buf.cross[stage - 2][r, h].astype(F32) + buf.crossed[stage - 2][r, h].astype(F32)

    dsl_copies = {}

    def second_norm(r, h):
        loaded(later.cot)
        total = crossed(2, r, h)
        at = pl.ds(h * 128, 128)
        second_in = buf.fo[r, at, :] + total + vec[5:6, :]
        center = second_in - mean_of(second_in)
        scale = lax.rsqrt(mean_of(center * center) + EPS)
        unit = center * scale

        @pl.when(chip == r)
        def _():
            layer = unit * vec[6:7, :] + vec[7:8, :]
            outs[0][at, :] = layer.astype(BF)

        grad = buf.cot[r, h].astype(F32)
        scaled = grad * vec[6:7, :]
        d_second = scale * (scaled - mean_of(scaled) - unit * mean_of(scaled * unit))
        buf.ds[r, at, :] = d_second
        buf.dsl[r, h, core] = d_second.astype(BF)
        own = buf.dsl.at[r, h, core]
        dsl_copies[r, h] = send(own, own, mate, (ROWS, r, h))
        buf.vs[0:1, :] += row_sum(grad * unit)
        buf.vs[1:2, :] += row_sum(grad)
        buf.vs[2:3, :] += row_sum(d_second)
        layer_rows.append((r, h))
        if len(layer_rows) == 2 * rows:
            emit(0)

    def ffn_backward(r, h):
        arrive(dsl_copies[r, h])
        rows_in = buf.dsl[r, h].reshape(256, 768)
        for part in range(3):
            at = pl.ds(part * 256, 256)
            d_hidden = dot(rows_in, buf.wd[at, :], 1, 1) * buf.gp[r, h, :, at]
            buf.vs[6:7, at] += row_sum(d_hidden)
            buf.dhl[r, h, :, at] = d_hidden.astype(BF)
        terms = dot(buf.dhl[r, h], buf.wu[...], 1, 1).astype(BF)
        buf.pair[1][r, h] = terms.reshape(2, 128, 768)
        pair_copies[3, r, h] = send(
            buf.pair[1].at[r, h, 1 - core], buf.paired[1].at[r, h], mate, (PAIR, r, h)
        )

    dal_copies = {}

    def first_norm_back(r, h):
        total = crossed(3, r, h)
        at = pl.ds(h * 128, 128)
        d_first = buf.ds[r, at, :] + total
        unit = buf.n1[r, at, :]
        scaled = d_first * vec[2:3, :]
        d_in = buf.r1[r, at, :] * (scaled - mean_of(scaled) - unit * mean_of(scaled * unit))
        buf.dfi[r, at, :] = d_in
        buf.dal[r, h, core] = d_in.astype(BF)
        own = buf.dal.at[r, h, core]
        dal_copies[r, h] = send(own, own, mate, (ROWS, r, h))
        buf.vs[3:4, :] += row_sum(d_first * unit)
        buf.vs[4:5, :] += row_sum(d_first)
        buf.vs[5:6, :] += row_sum(d_in)

    out_parts = []

    def attention_back(r):
        for h in range(2):
            arrive(dal_copies[r, h])
        buf.dctx[...] = dot(
            buf.dal[r].reshape(512, 768), buf.wo[me], 1, 1
        ).astype(BF)
        q_a = buf.mix[r, :, 0:128]
        k_a = buf.mix[r, :, 128:256]
        v_a = buf.mix[r, :, 256:384]
        qk_roll = buf.mixr[r]
        v_b = buf.mix[r, :, 512:640]
        d_q, d_k, d_v = [], [], []
        for head in range(3):
            tile = pl.ds((head // 2) * 128, 128)
            value = v_a if head < 2 else v_b
            for h in range(2):
                at = pl.ds(h * 256, 256)
                d_rows = buf.dctx[at, tile]
                if head == 0:
                    d_rows = jnp.where(low_half, d_rows, jnp.zeros_like(d_rows))
                if head == 1:
                    d_rows = jnp.where(low_half, jnp.zeros_like(d_rows), d_rows)
                probs = buf.prob[r, head, at, :]
                weighted = probs * dot(d_rows, value, 1, 1)
                inner = jnp.sum(weighted, axis=-1, keepdims=True)
                buf.dsc[head, at, :] = (weighted - probs * inner).astype(BF)
            d_scores = buf.dsc[head]
            d_q.append(dot(d_scores, k_a if head < 2 else qk_roll, 1, 0))
            d_k.append(dot(d_scores, q_a if head < 2 else qk_roll, 0, 0))
            d_v.append(dot(buf.prob[r, head].astype(BF), buf.dctx[:, tile], 0, 0))
        tiles = [
            jnp.where(lane_row, d_q[0], d_q[1]) * SCALE,
            jnp.where(lane_row, d_k[0], d_k[1]),
            jnp.where(lane_row, d_v[0], d_v[1]),
            jnp.where(lane_row, d_q[2] * SCALE, d_k[2]),
            jnp.where(lane_row, d_v[2], 0.0),
        ]
        for at, tile in enumerate(tiles):
            lanes = pl.ds(at * 128, 128)
            buf.dmx[r, :, lanes] = tile.astype(BF)
            if at != 1:
                buf.vs[7:8, lanes] += row_sum(tile)

    tok_copies = []

    def token_terms(r, h):
        terms = dot(
            buf.dmx[r, h * 256 : h * 256 + 256, :], buf.wq[...].reshape(640, 768), 1, 0
        )
        buf.pair[2][r, h] = terms.astype(BF).reshape(2, 128, 768)
        pair_copies[4, r, h] = send(
            buf.pair[2].at[r, h, 1 - core], buf.paired[2].at[r, h], mate, (PAIR, r, h)
        )

    cross4 = []

    def token_way():
        for h in range(2):
            cross4.append(remote(buf.x4.at[h], buf.x4r.at[h], over, (CROSS, 0, h)))

    def token_cross(r, h):
        if not cross4:
            token_way()
        pair_copies[4, r, h].wait_recv()

        @pl.when(chip != r)
        def _():
            own = buf.pair[2][r, h, core].astype(F32)
            other = buf.paired[2][r, h].astype(F32)
            buf.x4[h] = (own + other).astype(BF)
            cross4[h].start()

    def token_finish(h):
        cross4[h].wait_recv()
        own = buf.pair[2][chip, h, core].astype(F32)
        other = buf.paired[2][chip, h].astype(F32)
        pair = (own + other).astype(BF).astype(F32)
        total = pair + buf.x4r[h].astype(F32)
        result = buf.dfi[chip, pl.ds(h * 128, 128), :] + total
        outs[1][h * 128 : h * 128 + 128, :] = result.astype(BF)
        token_rows.append(h)
        if len(token_rows) == 2:
            emit(1)

    steps = {}
    starts = [sum(WIDTHS[:at]) for at in range(len(WIDTHS))]
    finished = []
    pieces = buf.pieces if fused else None

    def reduce_start(name):
        grad = gradient(name)
        width = WIDTHS[name]
        if not fused:
            outs[2][:, starts[name] : starts[name] + width] = grad
            finished.append(name)
            if len(finished) == len(WIDTHS):
                emit(2)
            return
        stage, came = pieces[name][:2]
        stage[...] = grad.astype(BF).reshape(stage.shape)
        if name in DEPTH_FIRST:
            steps[name] = send(stage.at[:, 1 - near], came, next_near, (-1, name))
        else:
            steps[name] = send(stage.at[:, :, 1 - why], came, side, (-1, name))

    def reduce_first(name):
        if not fused:
            return
        steps[name].wait_recv()
        stage, came, out, into = pieces[name][:4]
        for at in range(2):
            if name in DEPTH_FIRST:
                total = stage[1 - far, near, at].astype(F32) + came[1 - far, at].astype(F32)
            else:
                total = stage[at, 1 - near, why].astype(F32) + came[at, 1 - near].astype(F32)
            out[at] = total.astype(BF)
        steps[name] = send(
            out, into, next_far if name in DEPTH_FIRST else next_near, (-2, name)
        )

    def reduce_second(name):
        if not fused:
            return
        steps[name].wait_recv()
        stage, came, _, into, out, last = pieces[name]
        if name in DEPTH_FIRST:
            total = stage[far, near, 1 - why].astype(F32) + came[far, 1 - why].astype(F32)
            total = total + into[1 - why].astype(F32)
        else:
            total = stage[1 - far, near, why].astype(F32) + came[1 - far, near].astype(F32)
            total = total + into[1 - far].astype(F32)
        out[...] = total.astype(BF)
        steps[name] = send(out, last, side if name in DEPTH_FIRST else next_far, (-3, name))

    def emit(*which):
        for at in which:
            stored.append(fetch(outs[at], results[at], len(stored)))

    def reduce_finish(name):
        if not fused:
            return
        steps[name].wait_recv()
        stage, came, _, into, _, last = pieces[name]
        total = stage[far, near, why].astype(F32)
        if name in DEPTH_FIRST:
            total = total + came[far, why].astype(F32) + into[why].astype(F32)
        else:
            total = total + came[far, near].astype(F32) + into[far].astype(F32)
        total = total + last[...].astype(F32)
        flipped = None if name <= U2 else total.T
        if name <= D2:
            outs[10][:, starts[name] : starts[name] + 256] = total
        elif name <= U2:
            at = starts[name] - starts[U0]
            outs[8][:, at : at + 256] = total
        elif name == OUT:
            outs[4][0:128, :] = flipped
        elif name == QK:
            outs[2][0:128, :] = flipped[0:128]
            outs[2][192:320, :] = flipped[128:256]
        elif name == V:
            outs[2][384:512, :] = flipped
        elif name == QK2:
            outs[2][128:192, :] = flipped[0:64]
            outs[2][320:384, :] = flipped[64:128]
        else:
            outs[2][512:576, :] = flipped[0:64]
            outs[4][128:192, :] = flipped[64:128]
        before = set(finished)
        finished.append(name)
        after = set(finished)
        for group, at in (
            ({D0, D1, D2}, 10),
            ({U0, U1, U2}, 8),
            ({QK, V, QK2, V2}, 2),
            ({OUT, V2}, 4),
        ):
            if group <= after and not group <= before:
                emit(at)

    def down_grad(part):
        for r in range(rows):
            for h in range(2):
                arrive(dsl_copies[r, h])
        at = pl.ds(part * 256, 256)
        return dot(
            buf.dsl[...].reshape(rows * 512, 768),
            buf.act[:, :, :, at].reshape(rows * 512, 256),
            0,
            0,
        )

    def up_grad(part):
        at = pl.ds(part * 256, 256)
        return dot(
            buf.flow[...].reshape(rows * 512, 768),
            buf.dhl[:, :, :, at].reshape(rows * 512, 256),
            0,
            0,
        )

    def all_back():
        for r in range(rows):
            for h in range(2):
                arrive(dal_copies[r, h])

    def out_grad_first():
        all_back()
        return dot(
            buf.dal[...].reshape(rows * 512, 768),
            buf.ctx[:, :, 0:128].reshape(rows * 512, 128),
            0,
            0,
        )

    def out_grad_second():
        all_back()
        turned = dot(
            buf.dal[...].reshape(rows * 512, 768),
            buf.ctx[:, :, 128:256].reshape(rows * 512, 128),
            0,
            0,
        )
        return pltpu.roll(turned, 64, 1)

    def qkv_grad(low, high):
        return dot(
            buf.tok[...].reshape(rows * 512, 768),
            buf.dmx[:, :, low:high].reshape(rows * 512, high - low),
            0,
            0,
        )

    def gradient(name):
        if name <= D2:
            return down_grad(name)
        if name <= U2:
            return up_grad(name - U0)
        if name == OUT:
            return out_grad_first()
        if name == QK:
            return qkv_grad(0, 256)
        if name == V:
            return qkv_grad(256, 384)
        if name == QK2:
            return qkv_grad(384, 512)
        first = lax.broadcasted_iota(jnp.int32, (768, 128), 1) < 64
        return jnp.where(first, qkv_grad(512, 640), out_grad_second())

    small_copies = SimpleNamespace()

    def small_mate():
        small_copies.mate = send(buf.vs, buf.vm, mate, 3)

    def small_side():
        small_copies.mate.wait_recv()
        shared = lax.broadcasted_iota(jnp.int32, (8, 768), 0) < 6
        small = buf.vs[...] + jnp.where(shared, buf.vm[...], 0.0)
        if not fused:
            outs[3][...] = small
            emit(3)
            return
        buf.small[0][...] = small
        small_copies.side = send(buf.small[0], buf.small[1], side, 4)

    def small_near():
        if not fused:
            return
        small_copies.side.wait_recv()
        buf.small[2][...] = buf.small[0][...] + buf.small[1][...]
        small_copies.near = send(buf.small[2], buf.small[3], next_near, 5)

    def small_far():
        if not fused:
            return
        small_copies.near.wait_recv()
        buf.small[4][...] = buf.small[2][...] + buf.small[3][...]
        small_copies.far = send(buf.small[4], buf.small[5], next_far, 6)

    def small_finish():
        if not fused:
            return
        small_copies.far.wait_recv()
        small = buf.small[4][...] + buf.small[5][...]
        share = 768 // n_dp
        turned = pltpu.roll(small, 768 - dp * share, 1)
        for row, at in ((5, 5), (3, 6), (4, 7), (2, 11), (0, 12), (1, 13)):
            outs[at][...] = turned[row : row + 1, 0:share]
        wide = HEAD // n_dp
        lanes = lax.broadcasted_iota(jnp.int32, (8, 768), 1)
        depth = lax.broadcasted_iota(jnp.int32, (8, 768), 0)
        spread = jnp.where(lax.rem(lanes, HEAD) == depth + dp * wide, small[6:7, :], 0.0)
        group = lax.broadcasted_iota(jnp.int32, (768, 128), 0) // HEAD
        pick = (group == lax.broadcasted_iota(jnp.int32, (768, 128), 1)).astype(F32)
        outs[9][...] = jnp.dot(spread, pick, precision=lax.Precision.HIGHEST)[0:wide, 0:12]
        group = lanes // HEAD
        where = jnp.where(
            depth < 4,
            lax.rem(depth, 2) * 4 + depth // 2,
            jnp.where(depth == 4, 6, 8),
        )
        spread = jnp.where((group == where) & (depth < 6), small[7:8, :], 0.0)
        inside = lax.rem(lax.broadcasted_iota(jnp.int32, (768, 128), 0), HEAD)
        pick = (inside == lax.broadcasted_iota(jnp.int32, (768, 128), 1) + dp * wide).astype(F32)
        heads = jnp.dot(spread, pick, precision=lax.Precision.HIGHEST)
        for head in range(3):
            outs[3][head] = heads[head * 2 : head * 2 + 2, 0:wide]
        emit(3, 5, 6, 7, 9, 11, 12, 13)

    pl.semaphore_wait(barrier, len(partners))
    send_weight()
    prepare()
    project(0)
    attend(0, 1)
    send_context(0, 1)
    project(1)
    attend(1, 0)
    attend(1, 1)
    send_context(1, 1)
    forward_weight()
    attend(0, 0)
    send_context(0, 0)
    send_context(1, 0)
    complete_weight()
    first_norm(0, 1)
    ffn_forward(0, 1)
    first_norm(1, 1)
    exchange(2, 0, 1)
    first_norm(0, 0)
    ffn_forward(1, 1)
    ffn_forward(0, 0)
    first_norm(1, 0)
    exchange(2, 1, 1)
    exchange(2, 0, 0)
    ffn_forward(1, 0)
    second_norm(0, 1)
    exchange(2, 1, 0)
    ffn_backward(0, 1)
    exchange(3, 0, 1)
    second_norm(1, 1)
    ffn_backward(1, 1)
    second_norm(0, 0)
    exchange(3, 1, 1)
    ffn_backward(0, 0)
    exchange(3, 0, 0)
    second_norm(1, 0)
    reduce_start(D0)
    reduce_start(D1)
    reduce_start(D2)
    ffn_backward(1, 0)
    reduce_start(U2)
    first_norm_back(0, 1)
    reduce_start(U0)
    reduce_start(U1)
    exchange(3, 1, 0)
    first_norm_back(1, 1)
    reduce_first(D0)
    reduce_first(D1)
    first_norm_back(0, 0)
    reduce_first(U2)
    reduce_first(D2)
    attention_back(0)
    first_norm_back(1, 0)
    reduce_second(D1)
    token_terms(0, 1)
    reduce_second(D0)
    token_terms(0, 0)
    reduce_first(U0)
    reduce_start(OUT)
    attention_back(1)
    reduce_second(D2)
    reduce_start(V2)
    small_mate()
    token_cross(0, 1)
    token_cross(0, 0)
    reduce_start(QK)
    reduce_first(U1)
    reduce_finish(D0)
    reduce_start(V)
    reduce_finish(D1)
    reduce_second(U2)
    small_side()
    reduce_first(OUT)
    reduce_start(QK2)
    token_terms(1, 1)
    reduce_second(U0)
    token_terms(1, 0)
    reduce_first(V2)
    token_cross(1, 1)
    reduce_finish(D2)
    token_cross(1, 0)
    reduce_second(U1)
    reduce_second(OUT)
    reduce_first(QK)
    reduce_second(V2)
    reduce_finish(U0)
    reduce_first(V)
    token_finish(1)
    reduce_finish(U1)
    reduce_finish(U2)
    small_near()
    reduce_finish(OUT)
    reduce_second(QK)
    reduce_first(QK2)
    reduce_second(V)
    token_finish(0)
    small_far()
    reduce_finish(V2)
    reduce_second(QK2)
    reduce_finish(QK)
    reduce_finish(V)
    small_finish()
    reduce_finish(QK2)
    for copy in latest.values():
        copy.wait_send()
    for copy in stored:
        copy.wait()


def body(
    tokens,
    segment_ids,
    qkv_weight,
    qkv_bias,
    output_weight,
    output_bias,
    first_gain,
    first_shift,
    up_weight,
    up_bias,
    down_weight,
    down_bias,
    second_gain,
    second_shift,
    cotangent,
):
    rows = tokens.shape[0] // SEQ
    n_dp = lax.axis_size("dp")
    share = 768 // n_dp
    fused = n_dp == 8
    split = (rows, 2, 2, 128, 768)
    shape = jax.ShapeDtypeStruct
    outs = [shape((256, 768), BF), shape((256, 768), BF)]
    if fused:
        wide = HEAD // n_dp
        vector = shape((1, share), F32)
        outs += [
            shape((576, share), F32),
            shape((3, 2, wide), F32),
            shape((192, share), F32),
            vector,
            vector,
            vector,
            shape((share, 768), F32),
            shape((wide, 12), F32),
            shape((share, 768), F32),
            vector,
            vector,
            vector,
        ]
    else:
        outs += [shape((768, 2304), F32), shape((8, 768), F32)]
    plan = scratch_plan(rows, share, fused, outs)
    leaves, tree = jax.tree.flatten(plan, is_leaf=is_buffer)
    anywhere = pl.BlockSpec(memory_space=pl.ANY)

    def kernel(*refs):
        layer_kernel(rows, n_dp, fused, tree, *refs)

    got = pl.pallas_call(
        kernel,
        out_shape=outs,
        in_specs=[anywhere] * INPUTS,
        out_specs=[anywhere] * len(outs),
        scratch_shapes=[pltpu.VMEM(dims, kind) for dims, kind in leaves]
        + [
            pltpu.SemaphoreType.DMA((LOCAL_COPIES,)),
            pltpu.SemaphoreType.DMA((REMOTE_COPIES,)),
            pltpu.SemaphoreType.DMA((REMOTE_COPIES,)),
        ],
        compiler_params=pltpu.CompilerParams(
            collective_id=0, has_side_effects=True, vmem_limit_bytes=62 * 1024 * 1024
        ),
    )(
        tokens.reshape(split),
        cotangent.reshape(split),
        qkv_weight.transpose(1, 2, 3, 0).reshape(3, 192, 768),
        output_weight.reshape(192, 768),
        up_weight,
        down_weight,
        segment_ids,
        qkv_bias.transpose(1, 0, 2),
        up_bias,
        *(
            vector.reshape(6, 128)
            for vector in (
                output_bias,
                first_gain,
                first_shift,
                down_bias,
                second_gain,
                second_shift,
            )
        ),
    )
    if fused:
        got = hand_over(got)
    else:
        got = finish_plain(n_dp, *got)
    return (
        got[0],
        got[1],
        got[2].reshape(3, 3, HEAD, share).transpose(3, 0, 1, 2),
        got[3].transpose(1, 0, 2),
        got[4].reshape(3, HEAD, share),
        got[5].reshape(share),
        got[6].reshape(share),
        got[7].reshape(share),
        got[8],
        got[9].T,
        got[10].T,
        got[11].reshape(share),
        got[12].reshape(share),
        got[13].reshape(share),
    )


def hand_over(arrays):
    count = len(arrays)

    def kernel(*refs):
        source, result, held = (refs[at * count : at * count + count] for at in range(3))
        sem = refs[3 * count]
        inward = [
            pltpu.make_async_copy(source[at], held[at], sem.at[at]) for at in range(count)
        ]
        outward = [
            pltpu.make_async_copy(held[at], result[at], sem.at[count + at]) for at in range(count)
        ]
        for copy in inward:
            copy.start()
        for before, after in zip(inward, outward):
            before.wait()
            after.start()
        for copy in outward:
            copy.wait()

    anywhere = pl.BlockSpec(memory_space=pl.ANY)
    return pl.pallas_call(
        kernel,
        out_shape=[jax.ShapeDtypeStruct(a.shape, a.dtype) for a in arrays],
        in_specs=[anywhere] * count,
        out_specs=[anywhere] * count,
        scratch_shapes=[pltpu.VMEM(a.shape, a.dtype) for a in arrays]
        + [pltpu.SemaphoreType.DMA((2 * count,))],
    )(*arrays)


def finish_plain(n_dp, layer, tokens_grad, grads, small):
    share = 768 // n_dp
    grads = lax.psum_scatter(grads, "dp", scatter_dimension=0, tiled=True)
    small = lax.psum(small, "dp")
    dp = lax.axis_index("dp")
    wide = HEAD // n_dp
    turned = lax.dynamic_slice_in_dim(small, dp * share, share, 1)
    up_bias = lax.dynamic_slice_in_dim(small[6].reshape(12, HEAD), dp * wide, wide, 1)
    row = small[7]
    sums = jnp.stack(
        [row[0:64], row[256:320], row[64:128], row[320:384], row[384:448], row[512:576]]
    )
    sums = lax.dynamic_slice_in_dim(sums, dp * wide, wide, 1)
    down, up = grads[:, 0:768], grads[:, 768:1536]
    out_a, main, tail = grads[:, 1536:1664], grads[:, 1664:2048], grads[:, 2048:2304]
    qkv = jnp.concatenate(
        [
            main[:, 0:128],
            tail[:, 0:64],
            main[:, 128:256],
            tail[:, 64:128],
            main[:, 256:384],
            tail[:, 128:192],
        ],
        axis=1,
    )
    out = jnp.concatenate([out_a, tail[:, 192:256]], axis=1)
    return [
        layer,
        tokens_grad,
        qkv.T,
        sums.reshape(3, 2, wide),
        out.T,
        turned[5],
        turned[3],
        turned[4],
        up,
        up_bias.T,
        down,
        turned[2],
        turned[0],
        turned[1],
    ]


def solution(mesh):
    placed = (
        P("dp", None),
        P("dp", None),
        P(None, None, "tensor", None),
        P(None, "tensor", None),
        P("tensor", None, None),
        P(),
        P(),
        P(),
        P(None, "tensor"),
        P("tensor", None),
        P("tensor", None),
        P(),
        P(),
        P(),
        P("dp", None),
    )
    return jax.shard_map(
        body,
        mesh=mesh,
        in_specs=placed,
        out_specs=(
            P(("dp", "tensor"), None),
            P(("dp", "tensor"), None),
            P("dp", None, "tensor", None),
            P(None, "tensor", "dp"),
            P("tensor", None, "dp"),
            P("dp"),
            P("dp"),
            P("dp"),
            P("dp", "tensor"),
            P("tensor", "dp"),
            P("tensor", "dp"),
            P("dp"),
            P("dp"),
            P("dp"),
        ),
        check_vma=False,
    )
```

time: 99.3 us -> 91 us (0.916)
  Pallas kernels: 98.3 us -> 90 us
    pallas_call x1, Pallas kernels: 95.8 us -> 87.5 us  [body(): pl.pallas_call(kernel, out_shape=outs, in_specs=[anywhere] * INPUTS, out_...]
where the time goes in v3:
time: 91 us; the launch traced here: 90.8 us
  Pallas kernels  90 us (99%)
    pallas_call x1, Pallas kernels, body(): pl.pallas_call(kernel, out_shape=outs, in_specs=[anywhere] * INPUTS, out_...  87.5 us
    pallas_call x1, Pallas kernels, hand_over(): pl.pallas_call(kernel, out_shape=[jax.ShapeDtypeStruct(a.shape, a.dtype)...  2.48 us

profile of v3, /device:TPU:0, one launch (start us, length us, event | category | flops | bytes accessed | tf_op | source)
XLA Modules:
  0.0 90.8 jit_solution(3329037105196323251)
XLA Ops:
  0.7 87.5 %shard_map.254 = (bf16[256,768]{1,0:T(8,128)(2,1)}, bf16[256,768]{1,0:T(8,128)(2,1)}, f32[576,96]{1,0:T(8,128)}, f32[3,2,8]{2,1,0:T(2,128)}, f32[192,96]{1,0:T(8...) custom-call(bf16[2,2,2,128,768]{4,3,2,1,0:T(8,128)(2,1)} %bitcast.26, ...), custom_call_target="tpu_custom_call" | custom-call | tf_op jit(solution)/shard_map/pallas_call | solution.py:939
  88.2 2.5 %shard_map.255 = (bf16[256,768]{1,0:T(8,128)(2,1)}, bf16[256,768]{1,0:T(8,128)(2,1)}, f32[576,96]{1,0:T(8,128)}, f32[3,2,8]{2,1,0:T(2,128)}, f32[192,96]{1,0:T(8...) custom-call(bf16[256,768]{1,0:T(8,128)(2,1)} %get-tuple-element.42.r, ...), custom_call_target="tpu_custom_call" | custom-call | tf_op jit(solution)/shard_map/pallas_call | solution.py:1018

commit v4 on v3

--- a/solution.py
+++ b/solution.py
@@ -18,6 +18,7 @@
 D0, D1, D2, U0, U1, U2, OUT, QK, V, QK2, V2 = range(11)
 WIDTHS = (256, 256, 256, 256, 256, 256, 128, 256, 128, 128, 128)
 DEPTH_FIRST = (D0, U2)
+DIRECT = ()
 
 
 def dot(left, right, left_dim, right_dim):
@@ -64,8 +65,8 @@
         dhl=((rows, 2, 256, 768), BF),
         dfi=((rows, 256, 768), F32),
         dal=((rows, 2, 2, 128, 768), BF),
-        dctx=((512, 256), BF),
-        dsc=((3, 512, 512), BF),
+        dkv=((4, 512, 128), F32),
+        dq2=((512, 128), F32),
         dmx=((rows, 512, 640), BF),
         x4=((2, 128, 768), BF),
         x4r=((2, 128, 768), BF),
@@ -87,12 +88,12 @@
                 [
                     ((2, 2, 2, share, width), BF),
                     ((2, 2, share, width), BF),
-                    ((2, share, width), BF),
-                    ((2, share, width), BF),
+                    ((3 if name in DIRECT else 2, share, width), BF),
+                    ((3 if name in DIRECT else 2, share, width), BF),
                     ((share, width), BF),
                     ((share, width), BF),
                 ]
-                for width in WIDTHS
+                for name, width in enumerate(WIDTHS)
             ],
         )
     return plan
@@ -106,7 +107,7 @@
 OVER, CORNER, PAIR, ROWS, CROSS = range(5)
 FIRST_ROW = 0
 LOCAL_COPIES = 21
-REMOTE_COPIES = 60
+REMOTE_COPIES = 60 + len(DIRECT)
 
 
 def layer_kernel(rows, n_dp, fused, tree, *refs):
@@ -134,6 +135,7 @@
     side = (dp + 1 - 2 * why, me)
     next_near = (dp + 2 - 4 * near, me)
     next_far = (dp + 4 - 8 * far, me)
+    next_both = (dp + 6 - 4 * near - 8 * far, me)
 
     fetched = []
     stored, token_rows, layer_rows = [], [], []
@@ -187,7 +189,7 @@
 
     partners = [mate, over, over_mate]
     if fused:
-        partners += [side, next_near, next_far]
+        partners += [side, next_near, next_far] + [next_both] * bool(DIRECT)
     barrier = pltpu.get_barrier_semaphore()
     for device in partners:
         pl.semaphore_signal(barrier, inc=1, device_id=device, device_id_type=MESH_ID)
@@ -467,48 +469,60 @@
 
     out_parts = []
 
-    def attention_back(r):
-        for h in range(2):
-            arrive(dal_copies[r, h])
-        buf.dctx[...] = dot(
-            buf.dal[r].reshape(512, 768), buf.wo[me], 1, 1
-        ).astype(BF)
-        q_a = buf.mix[r, :, 0:128]
-        k_a = buf.mix[r, :, 128:256]
-        v_a = buf.mix[r, :, 256:384]
-        qk_roll = buf.mixr[r]
-        v_b = buf.mix[r, :, 512:640]
+    halves = []
+
+    def attend_back(r, h):
+        arrive(dal_copies[r, h])
+        at = pl.ds(h * 256, 256)
+        d_ctx = dot(buf.dal[r, h].reshape(256, 768), buf.wo[me], 1, 1).astype(BF)
+        turned = buf.mixr[r]
         d_q, d_k, d_v = [], [], []
         for head in range(3):
-            tile = pl.ds((head // 2) * 128, 128)
-            value = v_a if head < 2 else v_b
-            for h in range(2):
-                at = pl.ds(h * 256, 256)
-                d_rows = buf.dctx[at, tile]
-                if head == 0:
-                    d_rows = jnp.where(low_half, d_rows, jnp.zeros_like(d_rows))
-                if head == 1:
-                    d_rows = jnp.where(low_half, jnp.zeros_like(d_rows), d_rows)
-                probs = buf.prob[r, head, at, :]
-                weighted = probs * dot(d_rows, value, 1, 1)
-                inner = jnp.sum(weighted, axis=-1, keepdims=True)
-                buf.dsc[head, at, :] = (weighted - probs * inner).astype(BF)
-            d_scores = buf.dsc[head]
-            d_q.append(dot(d_scores, k_a if head < 2 else qk_roll, 1, 0))
-            d_k.append(dot(d_scores, q_a if head < 2 else qk_roll, 0, 0))
-            d_v.append(dot(buf.prob[r, head].astype(BF), buf.dctx[:, tile], 0, 0))
-        tiles = [
-            jnp.where(lane_row, d_q[0], d_q[1]) * SCALE,
+            tile = d_ctx[:, 0:128] if head < 2 else d_ctx[:, 128:256]
+            zero = jnp.zeros_like(tile)
+            rows_in = tile
+            if head == 0:
+                rows_in = jnp.where(low_half, tile, zero)
+            if head == 1:
+                rows_in = jnp.where(low_half, zero, tile)
+            value = buf.mix[r, :, 256:384] if head < 2 else buf.mix[r, :, 512:640]
+            probs = buf.prob[r, head, at, :]
+            weighted = probs * dot(rows_in, value, 1, 1)
+            inner = jnp.sum(weighted, axis=-1, keepdims=True)
+            d_scores = (weighted - probs * inner).astype(BF)
+            key = buf.mix[r, :, 128:256] if head < 2 else turned
+            query = buf.mix[r, at, 0:128] if head < 2 else buf.mixr[r, at, :]
+            d_q.append(dot(d_scores, key, 1, 0))
+            d_k.append(dot(d_scores, query, 0, 0))
+            d_v.append(dot(probs.astype(BF), tile, 0, 0))
+        query_rows = jnp.where(low_half, d_q[0], d_q[1]) * SCALE
+        buf.dmx[r, at, 0:128] = query_rows.astype(BF)
+        vs = buf.vs
+        vs[7:8, 0:128] += row_sum(query_rows)
+        buf.dq2[at, :] = d_q[2] * SCALE
+        sums = [
             jnp.where(lane_row, d_k[0], d_k[1]),
             jnp.where(lane_row, d_v[0], d_v[1]),
-            jnp.where(lane_row, d_q[2] * SCALE, d_k[2]),
-            jnp.where(lane_row, d_v[2], 0.0),
+            d_k[2],
+            d_v[2],
         ]
-        for at, tile in enumerate(tiles):
-            lanes = pl.ds(at * 128, 128)
+        halves.append(r)
+        if halves.count(r) < 2:
+            for part in range(4):
+                buf.dkv[part] = sums[part]
+            return
+        sums = [buf.dkv[part] + sums[part] for part in range(4)]
+        tiles = [
+            sums[0],
+            sums[1],
+            jnp.where(lane_row, buf.dq2[...], sums[2]),
+            jnp.where(lane_row, sums[3], 0.0),
+        ]
+        for part, tile in enumerate(tiles):
+            lanes = pl.ds(part * 128 + 128, 128)
             buf.dmx[r, :, lanes] = tile.astype(BF)
-            if at != 1:
-                buf.vs[7:8, lanes] += row_sum(tile)
+            if part > 0:
+                vs[7:8, lanes] += row_sum(tile)
 
     tok_copies = []
 
@@ -577,6 +591,19 @@
             return
         steps[name].wait_recv()
         stage, came, out, into = pieces[name][:4]
+        if name in DIRECT:
+            ways = (
+                (far, 1 - near, next_near),
+                (1 - far, near, next_far),
+                (1 - far, 1 - near, next_both),
+            )
+            copies = []
+            for at, (high, low, device) in enumerate(ways):
+                total = stage[high, low, why].astype(F32) + came[high, low].astype(F32)
+                out[at] = total.astype(BF)
+                copies.append(send(out.at[at], into.at[at], device, (-2 - at, name)))
+            steps[name] = copies
+            return
         for at in range(2):
             if name in DEPTH_FIRST:
                 total = stage[1 - far, near, at].astype(F32) + came[1 - far, at].astype(F32)
@@ -608,14 +635,21 @@
     def reduce_finish(name):
         if not fused:
             return
-        steps[name].wait_recv()
+        copies = steps[name] if name in DIRECT else [steps[name]]
+        for copy in copies:
+            copy.wait_recv()
         stage, came, _, into, _, last = pieces[name]
         total = stage[far, near, why].astype(F32)
         if name in DEPTH_FIRST:
             total = total + came[far, why].astype(F32) + into[why].astype(F32)
+        elif name in DIRECT:
+            total = total + came[far, near].astype(F32)
+            for at in range(3):
+                total = total + into[at].astype(F32)
         else:
             total = total + came[far, near].astype(F32) + into[far].astype(F32)
-        total = total + last[...].astype(F32)
+        if name not in DIRECT:
+            total = total + last[...].astype(F32)
         flipped = None if name <= U2 else total.T
         if name <= D2:
             outs[10][:, starts[name] : starts[name] + 256] = total
@@ -825,10 +859,12 @@
     first_norm_back(1, 1)
     reduce_first(D0)
     reduce_first(D1)
+    attend_back(0, 1)
     first_norm_back(0, 0)
     reduce_first(U2)
     reduce_first(D2)
-    attention_back(0)
+    attend_back(0, 0)
+    attend_back(1, 1)
     first_norm_back(1, 0)
     reduce_second(D1)
     token_terms(0, 1)
@@ -836,7 +872,7 @@
     token_terms(0, 0)
     reduce_first(U0)
     reduce_start(OUT)
-    attention_back(1)
+    attend_back(1, 0)
     reduce_second(D2)
     reduce_start(V2)
     small_mate()

time: 91 us -> 90.4 us (level)
  no operation moved by 1% of the time
where the time goes in v4:
time: 90.4 us; the launch traced here: 90.3 us
  Pallas kernels  89.4 us (99%)
    pallas_call x1, Pallas kernels, body(): pl.pallas_call(kernel, out_shape=outs, in_specs=[anywhere] * INPUTS, out_...  86.9 us
    pallas_call x1, Pallas kernels, hand_over(): pl.pallas_call(kernel, out_shape=[jax.ShapeDtypeStruct(a.shape, a.dtype)...  2.48 us

profile of v4, /device:TPU:0, one launch (start us, length us, event | category | flops | bytes accessed | tf_op | source)
XLA Modules:
  0.0 90.3 jit_solution(4100518078266133476)
XLA Ops:
  0.7 86.9 %shard_map.254 = (bf16[256,768]{1,0:T(8,128)(2,1)}, bf16[256,768]{1,0:T(8,128)(2,1)}, f32[576,96]{1,0:T(8,128)}, f32[3,2,8]{2,1,0:T(2,128)}, f32[192,96]{1,0:T(8...) custom-call(bf16[2,2,2,128,768]{4,3,2,1,0:T(8,128)(2,1)} %bitcast.26, ...), custom_call_target="tpu_custom_call" | custom-call | tf_op jit(solution)/shard_map/pallas_call | solution.py:975
  87.6 2.5 %shard_map.255 = (bf16[256,768]{1,0:T(8,128)(2,1)}, bf16[256,768]{1,0:T(8,128)(2,1)}, f32[576,96]{1,0:T(8,128)}, f32[3,2,8]{2,1,0:T(2,128)}, f32[192,96]{1,0:T(8...) custom-call(bf16[256,768]{1,0:T(8,128)(2,1)} %get-tuple-element.42.r, ...), custom_call_target="tpu_custom_call" | custom-call | tf_op jit(solution)/shard_map/pallas_call | solution.py:1054

commit v5 on v4

--- a/solution.py
+++ b/solution.py
@@ -878,19 +878,20 @@
     small_mate()
     token_cross(0, 1)
     token_cross(0, 0)
+    small_side()
     reduce_start(QK)
     reduce_first(U1)
     reduce_finish(D0)
     reduce_start(V)
     reduce_finish(D1)
     reduce_second(U2)
-    small_side()
     reduce_first(OUT)
     reduce_start(QK2)
     token_terms(1, 1)
     reduce_second(U0)
     token_terms(1, 0)
     reduce_first(V2)
+    small_near()
     token_cross(1, 1)
     reduce_finish(D2)
     token_cross(1, 0)
@@ -898,23 +899,22 @@
     reduce_second(OUT)
     reduce_first(QK)
     reduce_second(V2)
+    small_far()
     reduce_finish(U0)
     reduce_first(V)
     token_finish(1)
     reduce_finish(U1)
     reduce_finish(U2)
-    small_near()
     reduce_finish(OUT)
     reduce_second(QK)
     reduce_first(QK2)
     reduce_second(V)
     token_finish(0)
-    small_far()
     reduce_finish(V2)
+    small_finish()
     reduce_second(QK2)
     reduce_finish(QK)
     reduce_finish(V)
-    small_finish()
     reduce_finish(QK2)
     for copy in latest.values():
         copy.wait_send()

time: 90.4 us -> 90.9 us (level)
  no operation moved by 1% of the time
where the time goes in v5:
time: 90.9 us; the launch traced here: 90.8 us
  Pallas kernels  89.9 us (99%)
    pallas_call x1, Pallas kernels, body(): pl.pallas_call(kernel, out_shape=outs, in_specs=[anywhere] * INPUTS, out_...  87.5 us
    pallas_call x1, Pallas kernels, hand_over(): pl.pallas_call(kernel, out_shape=[jax.ShapeDtypeStruct(a.shape, a.dtype)...  2.48 us

profile of v5, /device:TPU:0, one launch (start us, length us, event | category | flops | bytes accessed | tf_op | source)
XLA Modules:
  0.0 90.8 jit_solution(10465123466091736337)
XLA Ops:
  0.7 87.5 %shard_map.254 = (bf16[256,768]{1,0:T(8,128)(2,1)}, bf16[256,768]{1,0:T(8,128)(2,1)}, f32[576,96]{1,0:T(8,128)}, f32[3,2,8]{2,1,0:T(2,128)}, f32[192,96]{1,0:T(8...) custom-call(bf16[2,2,2,128,768]{4,3,2,1,0:T(8,128)(2,1)} %bitcast.26, ...), custom_call_target="tpu_custom_call" | custom-call | tf_op jit(solution)/shard_map/pallas_call | solution.py:975
  88.1 2.5 %shard_map.255 = (bf16[256,768]{1,0:T(8,128)(2,1)}, bf16[256,768]{1,0:T(8,128)(2,1)}, f32[576,96]{1,0:T(8,128)}, f32[3,2,8]{2,1,0:T(2,128)}, f32[192,96]{1,0:T(8...) custom-call(bf16[256,768]{1,0:T(8,128)(2,1)} %get-tuple-element.42.r, ...), custom_call_target="tpu_custom_call" | custom-call | tf_op jit(solution)/shard_map/pallas_call | solution.py:1054
